TPU v7x, 32 devices: a whole 2x2x4 slice. The times are simulated.
32 devices in a mesh: segment: 2 (over core), expert: 16 (over z, y, x).
Axes of the slice: x: 2, y: 2, z: 4, core: 2. Of those that a mesh axis runs over, the one named last changes fastest.
Arguments:
- act_a: bfloat16 [2, 384, 2048], P('segment', 'expert'), may hold values from -6 to 6
- route_a1: int32 [2, 384, 8], P('segment', 'expert'), may hold values from 0 to 15, all different within a row; in each aligned block of 24 rows (0 to 23, 24 to 47, ..., all dimensions but the last counted through in order) at most 16 rows name the same one
- gate_a1: float32 [2, 384, 8], P('segment', 'expert'), may hold values from 0.1 to 0.5
- act_b1: bfloat16 [2, 384, 2048], P('segment', 'expert'), may hold values from -6 to 6
- route_b1: int32 [2, 384, 8], P('segment', 'expert'), may hold values from 0 to 15, all different within a row; in each aligned block of 24 rows (0 to 23, 24 to 47, ..., all dimensions but the last counted through in order) at most 16 rows name the same one
- gate_b1: float32 [2, 384, 8], P('segment', 'expert'), may hold values from 0.1 to 0.5
- grad_b1: bfloat16 [2, 384, 2048], P('segment', 'expert'), may hold values from -6 to 6
- act_b2: bfloat16 [2, 384, 2048], P('segment', 'expert'), may hold values from -6 to 6
- route_a2: int32 [2, 384, 8], P('segment', 'expert'), may hold values from 0 to 15, all different within a row; in each aligned block of 24 rows (0 to 23, 24 to 47, ..., all dimensions but the last counted through in order) at most 16 rows name the same one
- gate_a2: float32 [2, 384, 8], P('segment', 'expert'), may hold values from 0.1 to 0.5
- route_b2: int32 [2, 384, 8], P('segment', 'expert'), may hold values from 0 to 15, all different within a row; in each aligned block of 24 rows (0 to 23, 24 to 47, ..., all dimensions but the last counted through in order) at most 16 rows name the same one
- gate_b2: float32 [2, 384, 8], P('segment', 'expert'), may hold values from 0.1 to 0.5
- enter_a: bfloat16 [384, 2048], P('expert'), may hold values from -6 to 6
- enter_grad: bfloat16 [384, 2048], P('expert'), may hold values from -6 to 6
- w_gate: bfloat16 [2, 16, 2048, 768], P('segment', 'expert'), may hold values from -0.125 to 0.125
- w_up: bfloat16 [2, 16, 2048, 768], P('segment', 'expert'), may hold values from -0.125 to 0.125
- w_down: bfloat16 [2, 16, 768, 2048], P('segment', 'expert'), may hold values from -0.21875 to 0.21875
Outputs:
- fwd_one: bfloat16 [2, 384, 2048], P('segment', 'expert')
- grad_one: bfloat16 [2, 384, 2048], P('segment', 'expert')
- fwd_two: bfloat16 [2, 384, 2048], P('segment', 'expert')
- grad_two: bfloat16 [2, 384, 2048], P('segment', 'expert')
Inputs may be any that keep to these rules, and one draw needn't show every extreme that they name: `route_a1`: in each row the 8 experts differ; in the 24 rows of one device of one section no expert is named more than 16 times, a bound that some block reaches. `route_b1`: as for route_a1. `route_a2`: as for route_a1. `route_b2`: as for route_a1.
All inputs are finite; a program needn't handle non-finite values.
Results may differ from a plain program's by a relative error of at most 0.0085.
Values may be sent and summed in bfloat16 or wider, within the bound.
A program may use at most 128 MiB of HBM per device.

v0:
```python
import jax
import jax.numpy as jnp
from jax import lax
from jax.sharding import PartitionSpec as P

TOP = 8


def from_behind(block, axis, distance):
    devices = range(lax.axis_size(axis))
    route = [(i - distance, i) for i in devices if i - distance in devices]
    return lax.ppermute(block, axis, route)


def expert_forward(inputs, gate_mat, up_mat, down_mat):
    gate_pre = jnp.dot(inputs, gate_mat, preferred_element_type=jnp.float32)
    up_pre = jnp.dot(inputs, up_mat, preferred_element_type=jnp.float32)
    hidden = (jax.nn.silu(gate_pre) * up_pre).astype(jnp.bfloat16)
    return jnp.dot(hidden, down_mat, preferred_element_type=jnp.float32).astype(jnp.bfloat16)


def expert_backward(inputs, cotangent, gate_mat, up_mat, down_mat):
    gate_pre = jnp.dot(inputs, gate_mat, preferred_element_type=jnp.float32)
    up_pre = jnp.dot(inputs, up_mat, preferred_element_type=jnp.float32)
    sigma = jax.nn.sigmoid(gate_pre)
    d_hidden = jnp.dot(cotangent, down_mat.T, preferred_element_type=jnp.float32)
    d_gate = (d_hidden * up_pre * sigma * (1.0 + gate_pre * (1.0 - sigma))).astype(jnp.bfloat16)
    d_upper = (d_hidden * gate_pre * sigma).astype(jnp.bfloat16)
    total = jnp.dot(d_gate, gate_mat.T, preferred_element_type=jnp.float32)
    total = total + jnp.dot(d_upper, up_mat.T, preferred_element_type=jnp.float32)
    return total.astype(jnp.bfloat16)


def local_slots(route, capacity, experts):
    routed = route.reshape(-1)
    onehot = (routed[:, None] == jnp.arange(experts, dtype=jnp.int32)[None, :]).astype(jnp.int32)
    before = jnp.cumsum(onehot, axis=0) - onehot
    position = jnp.sum(before * onehot, axis=1)
    return routed * capacity + position


def collect(values, slots, capacity, experts):
    tok_rows = values.shape[0]
    chosen = slots[:, None] == jnp.arange(experts * capacity, dtype=jnp.int32)[None, :]
    select = chosen.reshape(tok_rows, TOP, experts * capacity).any(axis=1).astype(jnp.bfloat16)
    packed = jnp.einsum("tj,td->jd", select, values, preferred_element_type=jnp.float32)
    return packed.astype(jnp.bfloat16).reshape(experts, capacity, values.shape[1])


def spread(returned, slots, gates):
    width = returned.shape[2]
    picked = jnp.take(returned.reshape(-1, width), slots, axis=0).astype(jnp.float32)
    picked = picked.reshape(gates.shape[0], gates.shape[1], width)
    return jnp.sum(picked * gates[:, :, None], axis=1).astype(jnp.bfloat16)


def shards(
    act_a,
    route_a1,
    gate_a1,
    act_b1,
    route_b1,
    gate_b1,
    grad_b1,
    act_b2,
    route_a2,
    gate_a2,
    route_b2,
    gate_b2,
    enter_a,
    enter_grad,
    w_gate,
    w_up,
    w_down,
):
    experts = lax.axis_size("expert")
    tok_rows = act_a.shape[1]
    width = act_a.shape[2]
    capacity = 4 * tok_rows * TOP // (3 * experts)
    gate_mat = w_gate[0, 0]
    up_mat = w_up[0, 0]
    down_mat = w_down[0, 0]

    def run_forward(received):
        flat_in = received.reshape(-1, width)
        return expert_forward(flat_in, gate_mat, up_mat, down_mat).reshape(received.shape)

    def run_backward(received, cot_received):
        flat_in = received.reshape(-1, width)
        flat_cot = cot_received.reshape(-1, width)
        return expert_backward(flat_in, flat_cot, gate_mat, up_mat, down_mat).reshape(
            received.shape
        )

    def one_tick(fwd_in, fwd_route, fwd_gates, bwd_in, bwd_route, bwd_gates, bwd_cot):
        slots_fwd = local_slots(fwd_route, capacity, experts)
        slots_bwd = local_slots(bwd_route, capacity, experts)
        send_fwd = collect(fwd_in, slots_fwd, capacity, experts)
        send_inputs = collect(bwd_in, slots_bwd, capacity, experts)
        send_cot = collect(bwd_cot, slots_bwd, capacity, experts)
        back_fwd = lax.all_to_all(
            run_forward(
                lax.all_to_all(send_fwd, "expert", split_axis=0, concat_axis=0, tiled=True)
            ),
            "expert",
            split_axis=0,
            concat_axis=0,
            tiled=True,
        )
        back_bwd = lax.all_to_all(
            run_backward(
                lax.all_to_all(send_inputs, "expert", split_axis=0, concat_axis=0, tiled=True),
                lax.all_to_all(send_cot, "expert", split_axis=0, concat_axis=0, tiled=True),
            ),
            "expert",
            split_axis=0,
            concat_axis=0,
            tiled=True,
        )
        out_fwd = spread(back_fwd, slots_fwd, fwd_gates)
        out_bwd = spread(back_bwd, slots_bwd, bwd_gates)
        return (out_fwd[None], out_bwd[None])

    fwd_one, grad_one = one_tick(
        act_a[0], route_a1[0], gate_a1[0], act_b1[0], route_b1[0], gate_b1[0], grad_b1[0]
    )
    section = lax.axis_index("segment")
    moved_fwd = from_behind(fwd_one, "segment", 1)
    moved_grad = from_behind(grad_one, "segment", -1)
    in_two = jnp.where(section == 0, enter_a[None], moved_fwd)
    cot_two = jnp.where(section == lax.axis_size("segment") - 1, enter_grad[None], moved_grad)
    fwd_two, grad_two = one_tick(
        in_two[0], route_a2[0], gate_a2[0], act_b2[0], route_b2[0], gate_b2[0], cot_two[0]
    )
    return (fwd_one, grad_one, fwd_two, grad_two)


def solution(mesh):
    in_specs = (
        P("segment", "expert", None),
        P("segment", "expert", None),
        P("segment", "expert", None),
        P("segment", "expert", None),
        P("segment", "expert", None),
        P("segment", "expert", None),
        P("segment", "expert", None),
        P("segment", "expert", None),
        P("segment", "expert", None),
        P("segment", "expert", None),
        P("segment", "expert", None),
        P("segment", "expert", None),
        P("expert", None),
        P("expert", None),
        P("segment", "expert", None, None),
        P("segment", "expert", None, None),
        P("segment", "expert", None, None),
    )
    out_specs = (
        P("segment", "expert", None),
        P("segment", "expert", None),
        P("segment", "expert", None),
        P("segment", "expert", None),
    )
    return jax.shard_map(shards, mesh=mesh, in_specs=in_specs, out_specs=out_specs, check_vma=False)
```

profile of v0, /device:TPU:0, one launch (start us, length us, event | category | flops | bytes accessed | tf_op | source)
XLA Modules:
  0.0 310.4 jit_solution(16483439687804212381)
XLA Ops:
  5.3 8.4 %all-to-all-start.3 = ((bf16[16,16,2048]{2,1,0:T(8,128)(2,1)}), bf16[16,16,2048]{2,1,0:T(8,128)(2,1)}, u32[]{:S(2)}, u32[]{:S(2)}) async-start(bf16[16,16,2048]{2,1,0:T(8,128)(2,1)} %bitcast.232), calls=%async_computation.3 | async-start | bytes 2097152 | tf_op jit(solution)/shard_map/all_to_all | solution.py:112
  15.2 22.9 %all-to-all-done.3 = bf16[16,16,2048]{2,1,0:T(8,128)(2,1)} async-done(((bf16[16,16,2048]{2,1,0:T(8,128)(2,1)}), bf16[16,16,2048]{2,1,0:T(8,128)(2,1)}, u32[]{:S(2)}, u32[]{:S(2)}) %all-to-all-start.3) | async-done | bytes 1048608 | tf_op jit(solution)/shard_map/all_to_all | solution.py:112
  38.1 5.9 %all-to-all-start.2 = ((bf16[16,16,2048]{2,1,0:T(8,128)(2,1)}), bf16[16,16,2048]{2,1,0:T(8,128)(2,1)}, u32[]{:S(2)}, u32[]{:S(2)}) async-start(bf16[16,16,2048]{2,1,0:T(8,128)(2,1)} %bitcast.228), calls=%async_computation.2 | async-start | bytes 2097152 | tf_op jit(solution)/shard_map/all_to_all | solution.py:113
  46.9 20.2 %all-to-all-done.2 = bf16[16,16,2048]{2,1,0:T(8,128)(2,1)} async-done(((bf16[16,16,2048]{2,1,0:T(8,128)(2,1)}), bf16[16,16,2048]{2,1,0:T(8,128)(2,1)}, u32[]{:S(2)}, u32[]{:S(2)}) %all-to-all-start.2) | async-done | bytes 1048608 | tf_op jit(solution)/shard_map/all_to_all | solution.py:113
  67.1 6.1 %all-to-all-start.8 = ((bf16[16,16,2048]{2,1,0:T(8,128)(2,1)}), bf16[16,16,2048]{2,1,0:T(8,128)(2,1)}, u32[]{:S(2)}, u32[]{:S(2)}) async-start(bf16[16,16,2048]{2,1,0:T(8,128)(2,1)} %bitcast.229), calls=%async_computation.8 | async-start | bytes 2097152 | tf_op jit(solution)/shard_map/all_to_all | solution.py:112
  76.1 20.1 %all-to-all-done.8 = bf16[16,16,2048]{2,1,0:T(8,128)(2,1)} async-done(((bf16[16,16,2048]{2,1,0:T(8,128)(2,1)}), bf16[16,16,2048]{2,1,0:T(8,128)(2,1)}, u32[]{:S(2)}, u32[]{:S(2)}) %all-to-all-start.8) | async-done | bytes 1048608 | tf_op jit(solution)/shard_map/all_to_all | solution.py:112
  96.1 6.1 %all-to-all-start = ((bf16[16,16,2048]{2,1,0:T(8,128)(2,1)}), bf16[16,16,2048]{2,1,0:T(8,128)(2,1)}, u32[]{:S(2)}, u32[]{:S(2)}) async-start(bf16[16,16,2048]{2,1,0:T(8,128)(2,1)} %bitcast.231), calls=%async_computation | async-start | bytes 2097152 | tf_op jit(solution)/shard_map/all_to_all | solution.py:103
  111.5 6.5 %fusion.41 = bf16[256,2048]{1,0:T(8,128)(2,1)} fusion(f32[256,2048]{1,0:T(8,128)} %fusion.14, bf16[1,1,2048,768]{3,2,1,0:T(8,128)(2,1)} %param.33, f32[256,768]{1,0:T(8,128)} %copy-done.18, bf16[256,2048]{1,0:T(8,128)(2,1)} %bitcast.20, bf16[1,1,2048,768]{3,2,1,0:T(8,128)(2,1)S(1)} %copy-done, f32[256,768]{1,0:T(8,128)} %copy-done.17), kind=kOutput, calls=%fused_computation.39 | convolution fusion | flops 1613627392 | bytes 12058624 | tf_op jit(solution)/shard_map/dot_general | solution.py:29
  118.0 7.2 %all-to-all-done = bf16[16,16,2048]{2,1,0:T(8,128)(2,1)} async-done(((bf16[16,16,2048]{2,1,0:T(8,128)(2,1)}), bf16[16,16,2048]{2,1,0:T(8,128)(2,1)}, u32[]{:S(2)}, u32[]{:S(2)}) %all-to-all-start) | async-done | bytes 1048608 | tf_op jit(solution)/shard_map/all_to_all | solution.py:103
  125.1 6.1 %all-to-all-start.4 = ((bf16[16,16,2048]{2,1,0:T(8,128)(2,1)}), bf16[16,16,2048]{2,1,0:T(8,128)(2,1)}, u32[]{:S(2)}, u32[]{:S(2)}) async-start(bf16[16,16,2048]{2,1,0:T(8,128)(2,1)} %bitcast.235), calls=%async_computation.4 | async-start | bytes 2097152 | tf_op jit(solution)/shard_map/all_to_all | solution.py:110
  135.3 5.6 %fusion.44 = bf16[256,2048]{1,0:T(8,128)(2,1)} fusion(bf16[1,1,768,2048]{3,2,1,0:T(8,128)(2,1)} %param.35, bf16[256,2048]{1,0:T(8,128)(2,1)} %bitcast.4, bf16[1,1,2048,768]{3,2,1,0:T(8,128)(2,1)S(1)} %copy-done, f32[256,768]{1,0:T(8,128)} %fusion.30), kind=kOutput, calls=%fused_computation.46 | convolution fusion | flops 1612316672 | bytes 9175040 | tf_op jit(solution)/shard_map/dot_general | solution.py:19
  140.9 13.3 %all-to-all-done.4 = bf16[16,16,2048]{2,1,0:T(8,128)(2,1)} async-done(((bf16[16,16,2048]{2,1,0:T(8,128)(2,1)}), bf16[16,16,2048]{2,1,0:T(8,128)(2,1)}, u32[]{:S(2)}, u32[]{:S(2)}) %all-to-all-start.4) | async-done | bytes 1048608 | tf_op jit(solution)/shard_map/all_to_all | solution.py:110
  154.2 6.1 %all-to-all-start.1 = ((bf16[16,16,2048]{2,1,0:T(8,128)(2,1)}), bf16[16,16,2048]{2,1,0:T(8,128)(2,1)}, u32[]{:S(2)}, u32[]{:S(2)}) async-start(bf16[16,16,2048]{2,1,0:T(8,128)(2,1)} %bitcast.233), calls=%async_computation.1 | async-start | bytes 2097152 | tf_op jit(solution)/shard_map/all_to_all | solution.py:101
  171.7 11.5 %all-to-all-done.1 = bf16[16,16,2048]{2,1,0:T(8,128)(2,1)} async-done(((bf16[16,16,2048]{2,1,0:T(8,128)(2,1)}), bf16[16,16,2048]{2,1,0:T(8,128)(2,1)}, u32[]{:S(2)}, u32[]{:S(2)}) %all-to-all-start.1) | async-done | bytes 1048608 | tf_op jit(solution)/shard_map/all_to_all | solution.py:101
  183.2 6.1 %all-to-all-start.7 = ((bf16[16,16,2048]{2,1,0:T(8,128)(2,1)}), bf16[16,16,2048]{2,1,0:T(8,128)(2,1)}, u32[]{:S(2)}, u32[]{:S(2)}) async-start(bf16[16,16,2048]{2,1,0:T(8,128)(2,1)} %bitcast.227), calls=%async_computation.7 | async-start | bytes 2097152 | tf_op jit(solution)/shard_map/all_to_all | solution.py:113
  200.9 11.9 %all-to-all-done.7 = bf16[16,16,2048]{2,1,0:T(8,128)(2,1)} async-done(((bf16[16,16,2048]{2,1,0:T(8,128)(2,1)}), bf16[16,16,2048]{2,1,0:T(8,128)(2,1)}, u32[]{:S(2)}, u32[]{:S(2)}) %all-to-all-start.7) | async-done | bytes 1048608 | tf_op jit(solution)/shard_map/all_to_all | solution.py:113
  212.9 5.9 %all-to-all-start.5 = ((bf16[16,16,2048]{2,1,0:T(8,128)(2,1)}), bf16[16,16,2048]{2,1,0:T(8,128)(2,1)}, u32[]{:S(2)}, u32[]{:S(2)}) async-start(bf16[16,16,2048]{2,1,0:T(8,128)(2,1)} %bitcast.230), calls=%async_computation.5 | async-start | bytes 2097152 | tf_op jit(solution)/shard_map/all_to_all | solution.py:103
  228.0 6.5 %fusion.38 = bf16[256,2048]{1,0:T(8,128)(2,1)} fusion(f32[256,2048]{1,0:T(8,128)} %fusion.8, bf16[1,1,2048,768]{3,2,1,0:T(8,128)(2,1)} %param.33, f32[256,768]{1,0:T(8,128)} %copy-done.20, bf16[256,2048]{1,0:T(8,128)(2,1)} %bitcast.45, bf16[1,1,2048,768]{3,2,1,0:T(8,128)(2,1)S(1)} %copy-done, f32[256,768]{1,0:T(8,128)} %copy-done.19), kind=kOutput, calls=%fused_computation.38 | convolution fusion | flops 1613627392 | bytes 12058624 | tf_op jit(solution)/shard_map/dot_general | solution.py:29
  234.5 7.3 %all-to-all-done.5 = bf16[16,16,2048]{2,1,0:T(8,128)(2,1)} async-done(((bf16[16,16,2048]{2,1,0:T(8,128)(2,1)}), bf16[16,16,2048]{2,1,0:T(8,128)(2,1)}, u32[]{:S(2)}, u32[]{:S(2)}) %all-to-all-start.5) | async-done | bytes 1048608 | tf_op jit(solution)/shard_map/all_to_all | solution.py:103
  241.8 6.1 %all-to-all-start.9 = ((bf16[16,16,2048]{2,1,0:T(8,128)(2,1)}), bf16[16,16,2048]{2,1,0:T(8,128)(2,1)}, u32[]{:S(2)}, u32[]{:S(2)}) async-start(bf16[16,16,2048]{2,1,0:T(8,128)(2,1)} %bitcast.236), calls=%async_computation.9 | async-start | bytes 2097152 | tf_op jit(solution)/shard_map/all_to_all | solution.py:110
  252.1 5.6 %fusion.47 = bf16[256,2048]{1,0:T(8,128)(2,1)} fusion(bf16[1,1,768,2048]{3,2,1,0:T(8,128)(2,1)} %param.35, bf16[256,2048]{1,0:T(8,128)(2,1)} %bitcast.31, bf16[1,1,2048,768]{3,2,1,0:T(8,128)(2,1)S(1)} %copy-done, f32[256,768]{1,0:T(8,128)} %fusion.24), kind=kOutput, calls=%fused_computation.47 | convolution fusion | flops 1612316672 | bytes 9175040 | tf_op jit(solution)/shard_map/dot_general | solution.py:19
  257.7 13.4 %all-to-all-done.9 = bf16[16,16,2048]{2,1,0:T(8,128)(2,1)} async-done(((bf16[16,16,2048]{2,1,0:T(8,128)(2,1)}), bf16[16,16,2048]{2,1,0:T(8,128)(2,1)}, u32[]{:S(2)}, u32[]{:S(2)}) %all-to-all-start.9) | async-done | bytes 1048608 | tf_op jit(solution)/shard_map/all_to_all | solution.py:110
  271.1 6.0 %all-to-all-start.6 = ((bf16[16,16,2048]{2,1,0:T(8,128)(2,1)}), bf16[16,16,2048]{2,1,0:T(8,128)(2,1)}, u32[]{:S(2)}, u32[]{:S(2)}) async-start(bf16[16,16,2048]{2,1,0:T(8,128)(2,1)} %bitcast.234), calls=%async_computation.6 | async-start | bytes 2097152 | tf_op jit(solution)/shard_map/all_to_all | solution.py:101
  281.5 18.7 %all-to-all-done.6 = bf16[16,16,2048]{2,1,0:T(8,128)(2,1)} async-done(((bf16[16,16,2048]{2,1,0:T(8,128)(2,1)}), bf16[16,16,2048]{2,1,0:T(8,128)(2,1)}, u32[]{:S(2)}, u32[]{:S(2)}) %all-to-all-start.6) | async-done | bytes 1048608 | tf_op jit(solution)/shard_map/all_to_all | solution.py:101
  (132 shorter events, 75.8 us)
Async XLA Ops:
  0.6 108.5 %copy-start = (bf16[1,1,2048,768]{3,2,1,0:T(8,128)(2,1)S(1)}, bf16[1,1,2048,768]{3,2,1,0:T(8,128)(2,1)}, u32[]{:S(2)}) copy-start(bf16[1,1,2048,768]{3,2,1,0:T(8,128)(2,1)} %param.34) | copy-start | bytes 9437188
  2.9 41.2 %copy-start.8 = (s32[1,24,8]{1,2,0:T(8,128)S(1)}, s32[1,24,8]{1,2,0:T(8,128)}, u32[]{:S(2)}) copy-start(s32[1,24,8]{1,2,0:T(8,128)} %param.29) | copy-start | bytes 2308
  2.9 42.6 %copy-start.2 = (bf16[1,24,2048]{2,1,0:T(8,128)(2,1)S(1)}, bf16[1,24,2048]{2,1,0:T(8,128)(2,1)}, u32[]{:S(2)}) copy-start(bf16[1,24,2048]{2,1,0:T(8,128)(2,1)} %param.26) | copy-start | bytes 294916
  5.3 32.8 %all-to-all-start.3 = ((bf16[16,16,2048]{2,1,0:T(8,128)(2,1)}), bf16[16,16,2048]{2,1,0:T(8,128)(2,1)}, u32[]{:S(2)}, u32[]{:S(2)}) async-start(bf16[16,16,2048]{2,1,0:T(8,128)(2,1)} %bitcast.232), calls=%async_computation.3 | async-start | bytes 2097152 | tf_op jit(solution)/shard_map/all_to_all | solution.py:112
  13.7 59.5 %copy-start.9 = (s32[1,24,8]{1,2,0:T(8,128)S(1)}, s32[1,24,8]{1,2,0:T(8,128)}, u32[]{:S(2)}) copy-start(s32[1,24,8]{1,2,0:T(8,128)} %param.20) | copy-start | bytes 2308
  15.2 59.3 %copy-start.3 = (bf16[1,24,2048]{2,1,0:T(8,128)(2,1)S(1)}, bf16[1,24,2048]{2,1,0:T(8,128)(2,1)}, u32[]{:S(2)}) copy-start(bf16[1,24,2048]{2,1,0:T(8,128)(2,1)} %param.19) | copy-start | bytes 294916
  38.1 29.0 %all-to-all-start.2 = ((bf16[16,16,2048]{2,1,0:T(8,128)(2,1)}), bf16[16,16,2048]{2,1,0:T(8,128)(2,1)}, u32[]{:S(2)}, u32[]{:S(2)}) async-start(bf16[16,16,2048]{2,1,0:T(8,128)(2,1)} %bitcast.228), calls=%async_computation.2 | async-start | bytes 2097152 | tf_op jit(solution)/shard_map/all_to_all | solution.py:113
  67.1 29.0 %all-to-all-start.8 = ((bf16[16,16,2048]{2,1,0:T(8,128)(2,1)}), bf16[16,16,2048]{2,1,0:T(8,128)(2,1)}, u32[]{:S(2)}, u32[]{:S(2)}) async-start(bf16[16,16,2048]{2,1,0:T(8,128)(2,1)} %bitcast.229), calls=%async_computation.8 | async-start | bytes 2097152 | tf_op jit(solution)/shard_map/all_to_all | solution.py:112
  96.1 29.0 %all-to-all-start = ((bf16[16,16,2048]{2,1,0:T(8,128)(2,1)}), bf16[16,16,2048]{2,1,0:T(8,128)(2,1)}, u32[]{:S(2)}, u32[]{:S(2)}) async-start(bf16[16,16,2048]{2,1,0:T(8,128)(2,1)} %bitcast.231), calls=%async_computation | async-start | bytes 2097152 | tf_op jit(solution)/shard_map/all_to_all | solution.py:103
  125.1 29.0 %all-to-all-start.4 = ((bf16[16,16,2048]{2,1,0:T(8,128)(2,1)}), bf16[16,16,2048]{2,1,0:T(8,128)(2,1)}, u32[]{:S(2)}, u32[]{:S(2)}) async-start(bf16[16,16,2048]{2,1,0:T(8,128)(2,1)} %bitcast.235), calls=%async_computation.4 | async-start | bytes 2097152 | tf_op jit(solution)/shard_map/all_to_all | solution.py:110
  135.3 25.0 %copy-start.10 = (f32[1,24,8]{1,2,0:T(8,128)S(1)}, f32[1,24,8]{1,2,0:T(8,128)}, u32[]{:S(2)}) copy-start(f32[1,24,8]{1,2,0:T(8,128)} %param.24) | copy-start | bytes 2308
  154.2 29.0 %all-to-all-start.1 = ((bf16[16,16,2048]{2,1,0:T(8,128)(2,1)}), bf16[16,16,2048]{2,1,0:T(8,128)(2,1)}, u32[]{:S(2)}, u32[]{:S(2)}) async-start(bf16[16,16,2048]{2,1,0:T(8,128)(2,1)} %bitcast.233), calls=%async_computation.1 | async-start | bytes 2097152 | tf_op jit(solution)/shard_map/all_to_all | solution.py:101
  164.6 24.8 %copy-start.11 = (f32[1,24,8]{1,2,0:T(8,128)S(1)}, f32[1,24,8]{1,2,0:T(8,128)}, u32[]{:S(2)}) copy-start(f32[1,24,8]{1,2,0:T(8,128)} %param.21) | copy-start | bytes 2308
  164.6 24.8 %copy-start.12 = (s32[1,24,8]{1,2,0:T(8,128)S(1)}, s32[1,24,8]{1,2,0:T(8,128)}, u32[]{:S(2)}) copy-start(s32[1,24,8]{1,2,0:T(8,128)} %param.27) | copy-start | bytes 2308
  167.0 27.9 %copy-start.6 = (bf16[24,2048]{1,0:T(8,128)(2,1)}, bf16[24,2048]{1,0:T(8,128)(2,1)S(1)}, u32[]{:S(2)}) copy-start(bf16[24,2048]{1,0:T(8,128)(2,1)S(1)} %fusion.52) | copy-start | bytes 294916
  167.0 3.2 %collective-permute-start.1 = (bf16[1,24,2048]{2,1,0:T(8,128)(2,1)S(1)}, bf16[1,24,2048]{2,1,0:T(8,128)(2,1)S(1)}, u32[]{:S(2)}, u32[]{:S(2)}) collective-permute-start(bf16[1,24,2048]{2,1,0:T(8,128)(2,1)S(1)} %bitcast.237), channel_id=1, source_target_pairs={{16,0},{17,1},{18,2},{19,3},{20,4},{21,5},{22,6},{23,7},{24,8},{25... | collective-permute-start | bytes 294920 | tf_op jit(solution)/shard_map/ppermute | solution.py:12
  183.2 29.7 %all-to-all-start.7 = ((bf16[16,16,2048]{2,1,0:T(8,128)(2,1)}), bf16[16,16,2048]{2,1,0:T(8,128)(2,1)}, u32[]{:S(2)}, u32[]{:S(2)}) async-start(bf16[16,16,2048]{2,1,0:T(8,128)(2,1)} %bitcast.227), calls=%async_computation.7 | async-start | bytes 2097152 | tf_op jit(solution)/shard_map/all_to_all | solution.py:113
  197.2 24.9 %copy-start.7 = (bf16[24,2048]{1,0:T(8,128)(2,1)}, bf16[24,2048]{1,0:T(8,128)(2,1)S(1)}, u32[]{:S(2)}) copy-start(bf16[24,2048]{1,0:T(8,128)(2,1)S(1)} %fusion.53) | copy-start | bytes 294916
  197.3 2.2 collective-permute-start
  212.9 29.0 %all-to-all-start.5 = ((bf16[16,16,2048]{2,1,0:T(8,128)(2,1)}), bf16[16,16,2048]{2,1,0:T(8,128)(2,1)}, u32[]{:S(2)}, u32[]{:S(2)}) async-start(bf16[16,16,2048]{2,1,0:T(8,128)(2,1)} %bitcast.230), calls=%async_computation.5 | async-start | bytes 2097152 | tf_op jit(solution)/shard_map/all_to_all | solution.py:103
  241.8 29.2 %all-to-all-start.9 = ((bf16[16,16,2048]{2,1,0:T(8,128)(2,1)}), bf16[16,16,2048]{2,1,0:T(8,128)(2,1)}, u32[]{:S(2)}, u32[]{:S(2)}) async-start(bf16[16,16,2048]{2,1,0:T(8,128)(2,1)} %bitcast.236), calls=%async_computation.9 | async-start | bytes 2097152 | tf_op jit(solution)/shard_map/all_to_all | solution.py:110
  252.1 25.0 %copy-start.13 = (f32[1,24,8]{1,2,0:T(8,128)S(1)}, f32[1,24,8]{1,2,0:T(8,128)}, u32[]{:S(2)}) copy-start(f32[1,24,8]{1,2,0:T(8,128)} %param.30) | copy-start | bytes 2308
  252.1 25.1 %copy-start.14 = (f32[1,24,8]{1,2,0:T(8,128)S(1)}, f32[1,24,8]{1,2,0:T(8,128)}, u32[]{:S(2)}) copy-start(f32[1,24,8]{1,2,0:T(8,128)} %param.28) | copy-start | bytes 2308
  271.1 29.1 %all-to-all-start.6 = ((bf16[16,16,2048]{2,1,0:T(8,128)(2,1)}), bf16[16,16,2048]{2,1,0:T(8,128)(2,1)}, u32[]{:S(2)}, u32[]{:S(2)}) async-start(bf16[16,16,2048]{2,1,0:T(8,128)(2,1)} %bitcast.234), calls=%async_computation.6 | async-start | bytes 2097152 | tf_op jit(solution)/shard_map/all_to_all | solution.py:101
  (9 other events, 45.4 us)
where the time goes:
time: 312 us; the launch traced here: 310 us
  waiting for transfers between devices  149 us (48%)
  starting transfers between devices  65.4 us (21%)
  matrix products  58.7 us (19%)
  local copies, waits for them, and re-layouts  21.4 us (7%)
  other arithmetic  14.5 us (5%)
    all_to_all x2, waiting for transfers between devices, one_tick(): lax.all_to_all(send_inputs, 'expert', split_axis=0, concat_axis=0, tiled=...  43 us
    all_to_all x2, waiting for transfers between devices, one_tick(): lax.all_to_all(send_cot, 'expert', split_axis=0, concat_axis=0, tiled=True)  32.1 us
    all_to_all x2, waiting for transfers between devices, one_tick(): lax.all_to_all(run_forward(lax.all_to_all(send_fwd, 'expert', split_axis=...  30.2 us
    all_to_all x2, waiting for transfers between devices, one_tick(): lax.all_to_all(run_backward(lax.all_to_all(send_inputs, 'expert', split_a...  26.7 us
    gather x4, local copies, waits for them, and re-layouts, spread(): jnp.take(returned.reshape(-1, width), slots, axis=0).astype(jnp.float32)  16.7 us
    all_to_all x2, waiting for transfers between devices, one_tick(): lax.all_to_all(send_fwd, 'expert', split_axis=0, concat_axis=0, tiled=True)  14.5 us
    all_to_all x2, starting transfers between devices, one_tick(): lax.all_to_all(send_inputs, 'expert', split_axis=0, concat_axis=0, tiled=...  14.5 us
    dot_general x2, matrix products, expert_backward(): total = jnp.dot(d_gate, gate_mat.T, preferred_element_type=jnp.float32)  13 us
  transfers between devices with their start and end apart: 12, of which 12 were waited for; matrix products, arithmetic and copies ran while one was open for 25% of the time, Pallas kernels for 0%

commit v1 on v0

v1 whole, which is shorter than its diff:
```python
import jax
import jax.numpy as jnp
from jax import lax
from jax.sharding import PartitionSpec as P


def expert_forward(inputs, weight, gate_mat, up_mat, down_mat):
    gate_pre = jnp.dot(inputs, gate_mat, preferred_element_type=jnp.float32)
    up_pre = jnp.dot(inputs, up_mat, preferred_element_type=jnp.float32)
    hidden = (jax.nn.silu(gate_pre) * up_pre).astype(jnp.bfloat16)
    out = jnp.dot(hidden, down_mat, preferred_element_type=jnp.float32)
    return (out * weight[:, None]).astype(jnp.bfloat16)


def expert_backward(inputs, cotangent, weight, gate_mat, up_mat, down_mat):
    gate_pre = jnp.dot(inputs, gate_mat, preferred_element_type=jnp.float32)
    up_pre = jnp.dot(inputs, up_mat, preferred_element_type=jnp.float32)
    sigma = jax.nn.sigmoid(gate_pre)
    d_hidden = lax.dot_general(
        cotangent, down_mat, (((1,), (1,)), ((), ())), preferred_element_type=jnp.float32
    )
    d_gate = (d_hidden * up_pre * sigma * (1.0 + gate_pre * (1.0 - sigma))).astype(jnp.bfloat16)
    d_upper = (d_hidden * gate_pre * sigma).astype(jnp.bfloat16)
    dims = (((1,), (1,)), ((), ()))
    total = lax.dot_general(d_gate, gate_mat, dims, preferred_element_type=jnp.float32)
    total = total + lax.dot_general(d_upper, up_mat, dims, preferred_element_type=jnp.float32)
    return (total * weight[:, None]).astype(jnp.bfloat16)


def dense_gates(route, gates, experts):
    hit = route[:, :, None] == jnp.arange(experts, dtype=jnp.int32)[None, None, :]
    return jnp.sum(jnp.where(hit, gates[:, :, None], 0.0), axis=1)


def gather(block):
    return lax.all_gather(block, "expert", axis=0, tiled=True)


def scatter(block):
    return lax.psum_scatter(block, "expert", scatter_dimension=0, tiled=True)


def shards(
    act_a, route_a1, gate_a1, act_b1, route_b1, gate_b1, grad_b1, act_b2,
    route_a2, gate_a2, route_b2, gate_b2, enter_a, enter_grad, w_gate, w_up, w_down,
):
    experts = lax.axis_size("expert")
    sections = lax.axis_size("segment")
    section = lax.axis_index("segment")
    mine = lax.axis_index("expert")
    mats = (w_gate[0, 0], w_up[0, 0], w_down[0, 0])

    local = jnp.stack(
        [
            dense_gates(r[0], g[0], experts)
            for r, g in (
                (route_a1, gate_a1), (route_b1, gate_b1), (route_a2, gate_a2), (route_b2, gate_b2)
            )
        ],
        axis=0,
    )
    every = lax.all_gather(local, "expert", axis=1, tiled=True)
    weight = lax.dynamic_index_in_dim(every, mine, axis=2, keepdims=False)
    wa1, wb1, wa2, wb2 = weight[0], weight[1], weight[2], weight[3]

    x_a1 = gather(act_a[0])
    x_b1 = gather(act_b1[0])
    c_b1 = gather(grad_b1[0])
    x_b2 = gather(act_b2[0])

    fwd_one = scatter(expert_forward(x_a1, wa1, *mats))
    grad_one = scatter(expert_backward(x_b1, c_b1, wb1, *mats))

    if sections == 2:
        first = section == 0
        early = gather(jnp.where(first, enter_a, enter_grad))
        moved = lax.ppermute(jnp.where(first, fwd_one, grad_one), "segment", [(0, 1), (1, 0)])
        late = gather(moved)
        x_a2 = jnp.where(first, early, late)
        c_b2 = jnp.where(first, late, early)
    else:
        up = [(i, i + 1) for i in range(sections - 1)]
        down = [(i + 1, i) for i in range(sections - 1)]
        moved_fwd = lax.ppermute(fwd_one, "segment", up)
        moved_grad = lax.ppermute(grad_one, "segment", down)
        x_a2 = gather(jnp.where(section == 0, enter_a, moved_fwd))
        c_b2 = gather(jnp.where(section == sections - 1, enter_grad, moved_grad))

    fwd_two = scatter(expert_forward(x_a2, wa2, *mats))
    grad_two = scatter(expert_backward(x_b2, c_b2, wb2, *mats))
    return (fwd_one[None], grad_one[None], fwd_two[None], grad_two[None])


def solution(mesh):
    split = P("segment", "expert", None)
    weights = P("segment", "expert", None, None)
    in_specs = (split,) * 12 + (P("expert", None),) * 2 + (weights,) * 3
    out_specs = (split,) * 4
    return jax.shard_map(shards, mesh=mesh, in_specs=in_specs, out_specs=out_specs, check_vma=False)
```

time: 312 us -> 900 us (2.88)
  waiting for transfers between devices: 149 us -> 763 us
  starting transfers between devices: 65.4 us -> 0.87 us
  blocking collectives: 0 us -> 48 us
  local copies, waits for them, and re-layouts: 21.4 us -> 8.1 us
  between operations: 1.21 us -> 14.3 us
  other arithmetic: 14.5 us -> 4.46 us
    reduce_scatter x0 -> x4, waiting for transfers between devices: none -> 486 us  [scatter(): return lax.psum_scatter(block, 'expert', scatter_dimension=0, tiled=True)]
    all_gather x0 -> x6, waiting for transfers between devices: none -> 273 us  [gather(): return lax.all_gather(block, 'expert', axis=0, tiled=True)]
    all_to_all x10 -> x0, waiting for transfers between devices: 146 us -> none  [the longest x2 43 us: one_tick(): lax.all_to_all(send_inputs, 'expert', split_axis=0, concat_axis=0, tiled=...]
    all_to_all x10 -> x0, starting transfers between devices: 62.8 us -> none  [the longest x2 14.5 us: one_tick(): lax.all_to_all(send_inputs, 'expert', split_axis=0, concat_axis=0, tiled=...]
    all_gather x0 -> x1, blocking collectives: none -> 48 us  [shards(): every = lax.all_gather(local, 'expert', axis=1, tiled=True)]
    gather x4 -> x0, local copies, waits for them, and re-layouts: 16.7 us -> none  [spread(): jnp.take(returned.reshape(-1, width), slots, axis=0).astype(jnp.float32)]
    dot_general x14 -> x8, matrix products: 43.9 us -> 42.9 us  [the longest x2 16.5 us: expert_backward(): lax.dot_general(d_gate, gate_mat, dims, preferred_element_type=jnp.float32)]
  transfers between devices with their start and end apart: 12 -> 11, of which waited for: 12 -> 11; matrix products, arithmetic and copies ran while one was open for 25% -> 8% of each run, Pallas kernels for 0% -> 0%
where the time goes in v1:
time: 900 us; the launch traced here: 899 us
  waiting for transfers between devices  763 us (85%)
  matrix products  60.3 us (7%)
  blocking collectives  48 us (5%)
  between operations  14.3 us (2%)
    reduce_scatter x4, waiting for transfers between devices, scatter(): return lax.psum_scatter(block, 'expert', scatter_dimension=0, tiled=True)  486 us
    all_gather x6, waiting for transfers between devices, gather(): return lax.all_gather(block, 'expert', axis=0, tiled=True)  273 us
    all_gather x1, blocking collectives, shards(): every = lax.all_gather(local, 'expert', axis=1, tiled=True)  48 us
  transfers between devices with their start and end apart: 11, of which 11 were waited for; matrix products, arithmetic and copies ran while one was open for 8% of the time, Pallas kernels for 0%

profile of v1, /device:TPU:0, one launch (start us, length us, event | category | flops | bytes accessed | tf_op | source)
XLA Modules:
  0.0 899.3 jit_solution(13914803829861625159)
XLA Ops:
  12.4 48.0 %all_gather.22 = f32[4,384,16]{2,0,1:T(4,128)S(1)} all-gather(f32[4,24,16]{2,0,1:T(4,128)S(1)} %copy.45), channel_id=1, replica_groups=mesh['segment'=2,'expert'=16] {'expert'}, dimensions={1}, use_global_device_ids=true | all-gather | bytes 104448 | tf_op jit(solution)/shard_map/all_gather | solution.py:62
  60.5 6.2 dynamic-slice_reduce_fusion
  66.6 7.0 all-gather.15.cloned.1.call-done
  73.6 4.8 fusion.30
  78.4 6.9 multiply_convert_fusion.3
  85.6 47.5 %all-gather.17.cloned.1.call-done = bf16[1,384,2048]{2,1,0:T(8,128)(2,1)} async-done(((bf16[1,24,2048]{2,1,0:T(8,128)(2,1)}), bf16[1,384,2048]{2,1,0:T(8,128)(2,1)}) %all-gather.17.cloned.1.call-update) | async-done | bytes 1572880 | tf_op jit(solution)/shard_map/all_gather | solution.py:36
  133.1 4.9 fusion.4
  138.0 54.6 %all-gather.19.cloned.1.call-done = bf16[1,384,2048]{2,1,0:T(8,128)(2,1)} async-done(((bf16[1,24,2048]{2,1,0:T(8,128)(2,1)}), bf16[1,384,2048]{2,1,0:T(8,128)(2,1)}) %all-gather.19.cloned.1.call-update) | async-done | bytes 1572880 | tf_op jit(solution)/shard_map/all_gather | solution.py:36
  192.6 3.8 fusion.28
  196.4 3.1 fusion.14
  199.5 8.2 multiply_convert_fusion.2
  209.4 113.0 %reduce-scatter.5.cloned.1.call-done = bf16[24,2048]{1,0:T(8,128)(2,1)} async-done(((bf16[384,2048]{1,0:T(8,128)(2,1)}), bf16[24,2048]{1,0:T(8,128)(2,1)}) %reduce-scatter.5.cloned.1.call-update) | async-done | bytes 98320 | tf_op jit(solution)/shard_map/reduce_scatter | solution.py:40
  322.4 130.2 %reduce-scatter.7.cloned.1.call-done = bf16[24,2048]{1,0:T(8,128)(2,1)} async-done(((bf16[384,2048]{1,0:T(8,128)(2,1)}), bf16[24,2048]{1,0:T(8,128)(2,1)}) %reduce-scatter.7.cloned.1.call-update) | async-done | bytes 98320 | tf_op jit(solution)/shard_map/reduce_scatter | solution.py:40
  456.4 56.4 %all-gather.11.cloned.1.call-done = bf16[384,2048]{1,0:T(8,128)(2,1)} async-done(((bf16[24,2048]{1,0:T(8,128)(2,1)}), bf16[384,2048]{1,0:T(8,128)(2,1)}) %all-gather.11.cloned.1.call-update) | async-done | bytes 1572880 | tf_op jit(solution)/shard_map/all_gather | solution.py:36
  512.8 60.0 %all-gather.13.cloned.1.call-done = bf16[384,2048]{1,0:T(8,128)(2,1)} async-done(((bf16[24,2048]{1,0:T(8,128)(2,1)}), bf16[384,2048]{1,0:T(8,128)(2,1)}) %all-gather.13.cloned.1.call-update) | async-done | bytes 1572880 | tf_op jit(solution)/shard_map/all_gather | solution.py:36
  572.8 4.9 fusion.24
  577.7 6.9 multiply_convert_fusion.1
  584.9 47.4 %all-gather.21.cloned.1.call-done = bf16[1,384,2048]{2,1,0:T(8,128)(2,1)} async-done(((bf16[1,24,2048]{2,1,0:T(8,128)(2,1)}), bf16[1,384,2048]{2,1,0:T(8,128)(2,1)}) %all-gather.21.cloned.1.call-update) | async-done | bytes 1572880 | tf_op jit(solution)/shard_map/all_gather | solution.py:36
  632.3 3.9 fusion.22
  636.5 1.5 fusion
  638.1 3.1 fusion.8
  641.2 8.3 multiply_convert_fusion
  649.5 112.9 %reduce-scatter.9.cloned.1.call-done = bf16[24,2048]{1,0:T(8,128)(2,1)} async-done(((bf16[384,2048]{1,0:T(8,128)(2,1)}), bf16[24,2048]{1,0:T(8,128)(2,1)}) %reduce-scatter.9.cloned.1.call-update) | async-done | bytes 98320 | tf_op jit(solution)/shard_map/reduce_scatter | solution.py:40
  762.3 130.1 %reduce-scatter.11.cloned.1.call-done = bf16[24,2048]{1,0:T(8,128)(2,1)} async-done(((bf16[384,2048]{1,0:T(8,128)(2,1)}), bf16[24,2048]{1,0:T(8,128)(2,1)}) %reduce-scatter.11.cloned.1.call-update) | async-done | bytes 98320 | tf_op jit(solution)/shard_map/reduce_scatter | solution.py:40
  (52 shorter events, 11.4 us)
Async XLA Ops:
  7.2 71.2 %copy-start = (bf16[1,1,2048,768]{3,2,1,0:T(8,128)(2,1)S(1)}, bf16[1,1,2048,768]{3,2,1,0:T(8,128)(2,1)}, u32[]{:S(2)}) copy-start(bf16[1,1,2048,768]{3,2,1,0:T(8,128)(2,1)} %param.32) | copy-start | bytes 9437188
  7.2 66.4 %all-gather.15.cloned.1.call-start = ((), (), s32[]{:S(2)}) async-start(), calls=%async_computation.10 | async-start | bytes 1671168 | tf_op jit(solution)/shard_map/all_gather | solution.py:36
  7.9 125.2 %all-gather.17.cloned.1.call-start = ((), (), s32[]{:S(2)}) async-start(), calls=%async_computation.11 | async-start | bytes 1671168 | tf_op jit(solution)/shard_map/all_gather | solution.py:36
  8.7 183.9 %all-gather.19.cloned.1.call-start = ((), (), s32[]{:S(2)}) async-start(), calls=%async_computation.12 | async-start | bytes 1671168 | tf_op jit(solution)/shard_map/all_gather | solution.py:36
  9.4 313.0 %reduce-scatter.5.cloned.1.call-start = ((), (), s32[]{:S(2)}) async-start(), calls=%async_computation.4 | async-start | bytes 1671168 | tf_op jit(solution)/shard_map/reduce_scatter | solution.py:40
  85.3 367.3 %reduce-scatter.7.cloned.1.call-start = ((), (), s32[]{:S(2)}) async-start(), calls=%async_computation.5 | async-start | bytes 1671168 | tf_op jit(solution)/shard_map/reduce_scatter | solution.py:40
  192.6 3.8 copy-start.7
  196.4 3.1 copy-start.9
  207.7 0.9 copy-start.2
  207.7 0.9 copy-start.3
  207.8 305.0 %all-gather.11.cloned.1.call-start = ((), (), s32[]{:S(2)}) async-start(), calls=%async_computation.6 | async-start | bytes 1671168 | tf_op jit(solution)/shard_map/all_gather | solution.py:36
  209.4 363.5 %all-gather.13.cloned.1.call-start = ((), (), s32[]{:S(2)}) async-start(), calls=%async_computation.7 | async-start | bytes 1671168 | tf_op jit(solution)/shard_map/all_gather | solution.py:36
  453.6 1.4 collective-permute-start
  454.9 0.6 copy-start.1
  455.6 176.7 %all-gather.21.cloned.1.call-start = ((), (), s32[]{:S(2)}) async-start(), calls=%async_computation.13 | async-start | bytes 1671168 | tf_op jit(solution)/shard_map/all_gather | solution.py:36
  456.3 306.0 %reduce-scatter.9.cloned.1.call-start = ((), (), s32[]{:S(2)}) async-start(), calls=%async_computation.8 | async-start | bytes 1671168 | tf_op jit(solution)/shard_map/reduce_scatter | solution.py:40
  584.6 307.9 %reduce-scatter.11.cloned.1.call-start = ((), (), s32[]{:S(2)}) async-start(), calls=%async_computation.9 | async-start | bytes 1671168 | tf_op jit(solution)/shard_map/reduce_scatter | solution.py:40
  632.3 3.9 copy-start.4
  632.3 3.9 copy-start.5
  632.3 4.2 copy-start.6
  636.5 1.5 copy-start.8
  638.0 3.1 copy-start.10
Sparse Core Ops, SparseCore 0:
  10.8 62.7 all-gather.14
  76.4 56.6 all-gather.16
  135.9 56.6 all-gather.18
  197.8 124.6 reduce-scatter.4
  327.7 124.9 reduce-scatter.6
  455.8 56.8 all-gather.10
  516.1 56.6 all-gather.12
  575.6 56.6 all-gather.20
  637.7 124.6 reduce-scatter.8
  767.6 124.8 reduce-scatter.10

commit v2 on v0

--- a/solution.py
+++ b/solution.py
@@ -1,6 +1,8 @@
 import jax
 import jax.numpy as jnp
 from jax import lax
+from jax.experimental import pallas as pl
+from jax.experimental.pallas import tpu as pltpu
 from jax.sharding import PartitionSpec as P
 
 TOP = 8
@@ -54,7 +56,7 @@
     return jnp.sum(picked * gates[:, :, None], axis=1).astype(jnp.bfloat16)
 
 
-def shards(
+def slot_shards(
     act_a,
     route_a1,
     gate_a1,
@@ -135,30 +137,404 @@
     return (fwd_one, grad_one, fwd_two, grad_two)
 
 
+Z = 4
+Q = 4
+JOBS = 4
+BIG = 6
+TILE = 256
+LANES = 128
+MESH = pl.DeviceIdType.MESH
+F32 = jnp.float32
+BF16 = jnp.bfloat16
+
+
+def nt_dot(left, right):
+    return lax.dot_general(left, right, (((1,), (1,)), ((), ())), preferred_element_type=F32)
+
+
+def layer_kernel(
+    xs, wt, wg_h, wu_h, wd_h, out,
+    gath, gath_w, part, late, wg, wu, wd, h0, h1, wcol, d0, d1, rx, ry, sums, zin,
+    loc_sem, wsem, agz_s, agz_r, agl_s, agl_r, rsl_s, rsl_r, rsz_s, rsz_r, cross_s, cross_r,
+):
+    sec = lax.axis_index("segment")
+    me = lax.axis_index("expert")
+    z = me // Q
+    q = me % Q
+    x_pos = q % 2
+    y_pos = q // 2
+    qx = q + 1 - 2 * x_pos
+    qy = q + 2 - 4 * y_pos
+    qd = Q - 1 - q
+    x_peer = z * Q + qx
+    y_peer = z * Q + qy
+    width = xs.shape[2]
+    rows = xs.shape[1]
+    total = Q * Z * rows
+    half = width // 2
+    lo = pl.ds(0, half)
+    hi = pl.ds(half, half)
+    hidden = wg.shape[1]
+
+    def rcopy(src, dst, ssem, rsem, peer, seg=sec):
+        return pltpu.make_async_remote_copy(
+            src_ref=src, dst_ref=dst, send_sem=ssem, recv_sem=rsem,
+            device_id=(seg, peer), device_id_type=MESH,
+        )
+
+    barrier = pltpu.get_barrier_semaphore()
+    z_peers = [((z + j) % Z) * Q + q for j in range(1, Z)]
+    z_from = [(z + Z - j) % Z for j in range(1, Z)]
+    for peer in z_peers + [x_peer, y_peer]:
+        pl.semaphore_signal(barrier, inc=1, device_id=(sec, peer), device_id_type=MESH)
+    pl.semaphore_signal(barrier, inc=1, device_id=(1 - sec, me), device_id_type=MESH)
+
+    w_copies = [
+        pltpu.make_async_copy(src, dst, wsem.at[i])
+        for i, (src, dst) in enumerate(((wg_h, wg), (wu_h, wu), (wd_h, wd)))
+    ]
+    for c in w_copies:
+        c.start()
+
+    def buf(k):
+        return gath.at[k] if k < BIG else gath_w
+
+    def src(k):
+        return xs.at[k] if k < BIG - 1 else (late if k == BIG - 1 else wt)
+
+    def own_copy(k):
+        return pltpu.make_async_copy(src(k), buf(k).at[q, z], loc_sem.at[k])
+
+    def z_send(k, j):
+        return rcopy(src(k), buf(k).at[q, z], agz_s.at[k, j], agz_r.at[k, j], z_peers[j])
+
+    def z_recv(k, j):
+        return rcopy(src(k), buf(k).at[q, z_from[j]], agz_s.at[k, j], agz_r.at[k, j], z_peers[j])
+
+    def ag_start(k):
+        own_copy(k).start()
+        for j in range(Z - 1):
+            z_send(k, j).start()
+
+    def lay(k, i, block, cols, peer):
+        ref = buf(k).at[block] if cols is None else buf(k).at[block, :, :, cols]
+        return rcopy(ref, ref, agl_s.at[k, i], agl_r.at[k, i], peer)
+
+    def cols(k, c):
+        return c if k < BIG else None
+
+    def l1(k):
+        own_copy(k).wait()
+        for j in range(Z - 1):
+            z_recv(k, j).wait_recv()
+        lay(k, 0, q, None, x_peer).start()
+        lay(k, 1, q, None, y_peer).start()
+
+    def l2(k):
+        lay(k, 0, qx, None, x_peer).wait_recv()
+        lay(k, 2, qx, cols(k, lo), y_peer).start()
+        lay(k, 1, qy, None, y_peer).wait_recv()
+        if k < BIG:
+            lay(k, 3, qy, hi, x_peer).start()
+
+    def arrived(k):
+        lay(k, 2, qd, cols(k, lo), y_peer).wait_recv()
+        if k < BIG:
+            lay(k, 3, qd, hi, x_peer).wait_recv()
+
+    def ag_drain(k):
+        for j in range(Z - 1):
+            z_send(k, j).wait_send()
+        lay(k, 0, q, None, x_peer).wait_send()
+        lay(k, 1, q, None, y_peer).wait_send()
+        lay(k, 2, qx, cols(k, lo), y_peer).wait_send()
+        if k < BIG:
+            lay(k, 3, qy, hi, x_peer).wait_send()
+
+    def rs_copies(j):
+        def one(i, s, d, peer):
+            return rcopy(s, d, rsl_s.at[j, i], rsl_r.at[j, i], peer)
+
+        return (
+            one(0, part.at[j, qd, :, :, lo], d0.at[j], x_peer),
+            one(1, part.at[j, qd, :, :, hi], d1.at[j], y_peer),
+            one(2, part.at[j, qx], rx.at[j], x_peer),
+            one(3, part.at[j, qy], ry.at[j], y_peer),
+        )
+
+    def rs_z(j, i):
+        return rcopy(
+            sums.at[j, z_peers[i] // Q], zin.at[j, i], rsz_s.at[j, i], rsz_r.at[j, i], z_peers[i]
+        )
+
+    def s1(j):
+        a, b, _, _ = rs_copies(j)
+        a.start()
+        b.start()
+
+    def s2(j):
+        a, b, c, d = rs_copies(j)
+        a.wait_recv()
+        part[j, qy, :, :, lo] = (
+            part[j, qy, :, :, lo].astype(F32) + d0[j].astype(F32)
+        ).astype(BF16)
+        d.start()
+        b.wait_recv()
+        part[j, qx, :, :, hi] = (
+            part[j, qx, :, :, hi].astype(F32) + d1[j].astype(F32)
+        ).astype(BF16)
+        c.start()
+
+    def s3(j):
+        _, _, c, d = rs_copies(j)
+        c.wait_recv()
+        d.wait_recv()
+        for i in range(Z - 1):
+            zz = z_peers[i] // Q
+            sums[j, zz] = (
+                part[j, q, zz].astype(F32) + rx[j, zz].astype(F32) + ry[j, zz].astype(F32)
+            ).astype(BF16)
+            rs_z(j, i).start()
+
+    def fin(j):
+        for i in range(Z - 1):
+            rs_z(j, i).wait_recv()
+        acc = part[j, q, z].astype(F32) + rx[j, z].astype(F32) + ry[j, z].astype(F32)
+        for i in range(Z - 1):
+            acc = acc + zin[j, i].astype(F32)
+        out[j] = acc.astype(BF16)
+
+    def rs_drain(j):
+        for c in rs_copies(j):
+            c.wait_send()
+        for i in range(Z - 1):
+            rs_z(j, i).wait_send()
+
+    def crossing():
+        return rcopy(out.at[0], late, cross_s, cross_r, me, 1 - sec)
+
+    def tile(n):
+        return pl.ds(pl.multiple_of(n * TILE, TILE), TILE)
+
+    def part_a(j, is_f):
+        lane = lax.broadcasted_iota(jnp.int32, (total, LANES), 1)
+        table = gath_w[...].reshape(total, LANES)
+        picked = jnp.sum(jnp.where(lane == j * (Q * Z) + me, table, 0.0), axis=1, keepdims=True)
+        wcol[...] = jnp.broadcast_to(picked, (total, LANES))
+
+        @pl.when(is_f)
+        def _():
+            xi = j + (j + 1) // 2
+
+            def body(n, carry):
+                x = gath[xi].reshape(total, width)
+                g = jnp.dot(x, wg[:, tile(n)], preferred_element_type=F32)
+                u = jnp.dot(x, wu[:, tile(n)], preferred_element_type=F32)
+                h0[:, tile(n)] = (g * jax.nn.sigmoid(g) * u).astype(BF16)
+                return carry
+
+            lax.fori_loop(0, hidden // TILE, body, 0)
+
+        @pl.when(jnp.logical_not(is_f))
+        def _():
+            xi = jnp.where(j >= 2, 4, j)
+            ci = j + 1 + j // 3
+
+            def body(n, carry):
+                x = gath[xi].reshape(total, width)
+                c = gath[ci].reshape(total, width)
+                g = jnp.dot(x, wg[:, tile(n)], preferred_element_type=F32)
+                u = jnp.dot(x, wu[:, tile(n)], preferred_element_type=F32)
+                dh = nt_dot(c, wd[tile(n), :])
+                sig = jax.nn.sigmoid(g)
+                h0[:, tile(n)] = (dh * u * sig * (1.0 + g * (1.0 - sig))).astype(BF16)
+                h1[:, tile(n)] = (dh * g * sig).astype(BF16)
+                return carry
+
+            lax.fori_loop(0, hidden // TILE, body, 0)
+
+    def part_b(j, is_f):
+        def put(n, o):
+            w = jnp.concatenate([wcol[...]] * (TILE // LANES), axis=1)
+            part[j, :, :, :, tile(n)] = (o * w).astype(BF16).reshape(Q, Z, rows, TILE)
+
+        @pl.when(is_f)
+        def _():
+            def body(n, carry):
+                put(n, jnp.dot(h0[...], wd[:, tile(n)], preferred_element_type=F32))
+                return carry
+
+            lax.fori_loop(0, width // TILE, body, 0)
+
+        @pl.when(jnp.logical_not(is_f))
+        def _():
+            def body(n, carry):
+                put(n, nt_dot(h0[...], wg[tile(n), :]) + nt_dot(h1[...], wu[tile(n), :]))
+                return carry
+
+            lax.fori_loop(0, width // TILE, body, 0)
+
+    pl.semaphore_wait(barrier, Z + 2)
+    W = BIG
+    for k in (0, 1, W, 2, 3, 4):
+        ag_start(k)
+    l1(0)
+    l1(1)
+    l1(W)
+    l2(0)
+    l1(2)
+    l2(1)
+    l2(W)
+    arrived(0)
+    for c in w_copies:
+        c.wait()
+    arrived(1)
+    arrived(W)
+
+    def mid_0():
+        l2(2)
+        l1(3)
+
+    def end_0():
+        s1(0)
+        arrived(2)
+
+    def mid_1():
+        s2(0)
+        l2(3)
+
+    def end_1():
+        s1(1)
+        l1(4)
+        s3(0)
+        arrived(3)
+        s2(1)
+        l2(4)
+        fin(0)
+        crossing().start()
+        crossing().wait_recv()
+        ag_start(5)
+        arrived(4)
+
+    def mid_2():
+        s3(1)
+        l1(5)
+
+    def end_2():
+        s1(2)
+        l2(5)
+        fin(1)
+        s2(2)
+        arrived(5)
+
+    def mid_3():
+        s3(2)
+
+    def end_3():
+        s1(3)
+        s2(3)
+        fin(2)
+        s3(3)
+        fin(3)
+
+    mids = (mid_0, mid_1, mid_2, mid_3)
+    ends = (end_0, end_1, end_2, end_3)
+
+    def job(j, carry):
+        is_f = (sec + j) % 2 == 0
+        part_a(j, is_f)
+        for i, fn in enumerate(mids):
+            pl.when(j == i)(fn)
+        part_b(j, is_f)
+        for i, fn in enumerate(ends):
+            pl.when(j == i)(fn)
+        return carry
+
+    lax.fori_loop(0, JOBS, job, 0)
+
+    for k in range(BIG + 1):
+        ag_drain(k)
+    for j in range(JOBS):
+        rs_drain(j)
+    crossing().wait_send()
+
+
+def fused_shards(
+    act_a, route_a1, gate_a1, act_b1, route_b1, gate_b1, grad_b1, act_b2,
+    route_a2, gate_a2, route_b2, gate_b2, enter_a, enter_grad, w_gate, w_up, w_down,
+):
+    experts = lax.axis_size("expert")
+    first = lax.axis_index("segment") == 0
+    rows, width = act_a.shape[1:]
+    hidden = w_gate.shape[3]
+
+    def pick(one, two):
+        return jnp.where(first, one, two)
+
+    xs = jnp.stack(
+        [
+            pick(act_a[0], act_b1[0]),
+            pick(act_b1[0], grad_b1[0]),
+            pick(grad_b1[0], act_a[0]),
+            pick(enter_a, enter_grad),
+            act_b2[0],
+        ],
+        axis=0,
+    )
+    pairs = ((route_a1, gate_a1), (route_b1, gate_b1), (route_a2, gate_a2), (route_b2, gate_b2))
+    route = jnp.stack([pick(pairs[j][0][0], pairs[j ^ 1][0][0]) for j in range(JOBS)], axis=1)
+    gate = jnp.stack([pick(pairs[j][1][0], pairs[j ^ 1][1][0]) for j in range(JOBS)], axis=1)
+    hit = route[:, :, :, None] == jnp.arange(experts, dtype=jnp.int32)
+    dense = jnp.sum(jnp.where(hit, gate[:, :, :, None], 0.0), axis=2)
+    wt = jnp.pad(dense.reshape(rows, JOBS * experts), ((0, 0), (0, LANES - JOBS * experts)))
+
+    vmem = pl.BlockSpec(memory_space=pltpu.VMEM)
+    hbm = pl.BlockSpec(memory_space=pl.ANY)
+    dma = pltpu.SemaphoreType.DMA
+    total = experts * rows
+    done = pl.pallas_call(
+        layer_kernel,
+        out_shape=jax.ShapeDtypeStruct((JOBS, rows, width), BF16),
+        in_specs=[vmem, vmem, hbm, hbm, hbm],
+        out_specs=vmem,
+        scratch_shapes=[
+            pltpu.VMEM((BIG, Q, Z, rows, width), BF16),
+            pltpu.VMEM((Q, Z, rows, LANES), F32),
+            pltpu.VMEM((JOBS, Q, Z, rows, width), BF16),
+            pltpu.VMEM((rows, width), BF16),
+            pltpu.VMEM((width, hidden), BF16),
+            pltpu.VMEM((width, hidden), BF16),
+            pltpu.VMEM((hidden, width), BF16),
+            pltpu.VMEM((total, hidden), BF16),
+            pltpu.VMEM((total, hidden), BF16),
+            pltpu.VMEM((total, LANES), F32),
+            pltpu.VMEM((JOBS, Z, rows, width // 2), BF16),
+            pltpu.VMEM((JOBS, Z, rows, width // 2), BF16),
+            pltpu.VMEM((JOBS, Z, rows, width), BF16),
+            pltpu.VMEM((JOBS, Z, rows, width), BF16),
+            pltpu.VMEM((JOBS, Z, rows, width), BF16),
+            pltpu.VMEM((JOBS, Z - 1, rows, width), BF16),
+            dma((BIG + 1,)), dma((3,)),
+            dma((BIG + 1, Z - 1)), dma((BIG + 1, Z - 1)),
+            dma((BIG + 1, 4)), dma((BIG + 1, 4)),
+            dma((JOBS, 4)), dma((JOBS, 4)),
+            dma((JOBS, Z - 1)), dma((JOBS, Z - 1)),
+            dma, dma,
+        ],
+        compiler_params=pltpu.CompilerParams(
+            collective_id=0, has_side_effects=True, vmem_limit_bytes=60 * 1024 * 1024
+        ),
+    )(xs, wt, w_gate[0, 0], w_up[0, 0], w_down[0, 0])
+    fwd_one, grad_one = pick(done[0], done[1]), pick(done[1], done[0])
+    fwd_two, grad_two = pick(done[2], done[3]), pick(done[3], done[2])
+    return (fwd_one[None], grad_one[None], fwd_two[None], grad_two[None])
+
+
 def solution(mesh):
-    in_specs = (
-        P("segment", "expert", None),
-        P("segment", "expert", None),
-        P("segment", "expert", None),
-        P("segment", "expert", None),
-        P("segment", "expert", None),
-        P("segment", "expert", None),
-        P("segment", "expert", None),
-        P("segment", "expert", None),
-        P("segment", "expert", None),
-        P("segment", "expert", None),
-        P("segment", "expert", None),
-        P("segment", "expert", None),
-        P("expert", None),
-        P("expert", None),
-        P("segment", "expert", None, None),
-        P("segment", "expert", None, None),
-        P("segment", "expert", None, None),
-    )
-    out_specs = (
-        P("segment", "expert", None),
-        P("segment", "expert", None),
-        P("segment", "expert", None),
-        P("segment", "expert", None),
-    )
-    return jax.shard_map(shards, mesh=mesh, in_specs=in_specs, out_specs=out_specs, check_vma=False)
+    split = P("segment", "expert", None)
+    weights = P("segment", "expert", None, None)
+    in_specs = (split,) * 12 + (P("expert", None),) * 2 + (weights,) * 3
+    out_specs = (split,) * 4
+    fits = mesh.shape["segment"] == 2 and mesh.shape["expert"] == Q * Z
+    body = fused_shards if fits else slot_shards
+    return jax.shard_map(body, mesh=mesh, in_specs=in_specs, out_specs=out_specs, check_vma=False)

time: 312 us -> 186 us (0.60)
  Pallas kernels: 0 us -> 176 us
  waiting for transfers between devices: 149 us -> 0 us
  starting transfers between devices: 65.4 us -> 0 us
  matrix products: 58.7 us -> 0 us
  local copies, waits for them, and re-layouts: 21.4 us -> 1.59 us
  other arithmetic: 14.5 us -> 7.19 us
    pallas_call x0 -> x1, Pallas kernels: none -> 176 us  [fused_shards(): pl.pallas_call(layer_kernel, out_shape=jax.ShapeDtypeStruct((JOBS, rows,...]
    all_to_all x10 -> x0, waiting for transfers between devices: 146 us -> none  [the longest x2 43 us: one_tick(): lax.all_to_all(send_inputs, 'expert', split_axis=0, concat_axis=0, tiled=...]
    all_to_all x10 -> x0, starting transfers between devices: 62.8 us -> none  [the longest x2 14.5 us: one_tick(): lax.all_to_all(send_inputs, 'expert', split_axis=0, concat_axis=0, tiled=...]
    dot_general x18 -> x0, matrix products: 58.7 us -> none  [the longest x2 13 us: expert_backward(): total = jnp.dot(d_gate, gate_mat.T, preferred_element_type=jnp.float32)]
    gather x4 -> x0, local copies, waits for them, and re-layouts: 16.7 us -> none  [spread(): jnp.take(returned.reshape(-1, width), slots, axis=0).astype(jnp.float32)]
    reduce_sum x8 -> x1, other arithmetic: 11 us -> 0.04 us  [fused_shards(): dense = jnp.sum(jnp.where(hit, gate[:, :, :, None], 0.0), axis=2)]
    unnamed x0 -> x4, other arithmetic: none -> 3.72 us
    select_n x0 -> x3, other arithmetic: none -> 3.42 us  [pick(): return jnp.where(first, one, two)]
  transfers between devices with their start and end apart: 12 -> 0, of which waited for: 12 -> 0; matrix products, arithmetic and copies ran while one was open for 25% -> 0% of each run, Pallas kernels for 0% -> 0%
where the time goes in v2:
time: 186 us; the launch traced here: 185 us
  Pallas kernels  176 us (95%)
  other arithmetic  7.19 us (4%)
    pallas_call x1, Pallas kernels, fused_shards(): pl.pallas_call(layer_kernel, out_shape=jax.ShapeDtypeStruct((JOBS, rows,...  176 us

profile of v2, /device:TPU:0, one launch (start us, length us, event | category | flops | bytes accessed | tf_op | source)
XLA Modules:
  0.0 185.2 jit_solution(11792115766520310163)
XLA Ops:
  0.6 0.9 select_dynamic-update-slice_fusion.2
  1.6 0.9 select_dynamic-update-slice_fusion.1
  2.5 0.9 select_dynamic-update-slice_fusion
  3.4 0.9 bitcast_dynamic-update-slice_fusion
  4.4 0.9 constant_dynamic-update-slice_fusion.xs
  5.3 0.0 copy-start
  5.3 0.9 select_bitcast_fusion.1
  6.2 0.7 select_bitcast_fusion.5
  7.0 0.1 copy.26
  7.0 0.6 pad.4.wt
  7.6 0.0 copy-done
  7.6 175.8 %shard_map.192 = bf16[4,24,2048]{2,1,0:T(8,128)(2,1)} custom-call(bf16[5,24,2048]{2,1,0:T(8,128)(2,1)} %copy-done, f32[24,128]{1,0:T(8,128)} %pad.4.wt, bf16[2048,768]{1,0:T(8,128)(2,1)} %bitcast.22, bf16[2048,768]{1,0:T(8,128)(2,1)} %bitcast.23, bf16[768,2048]{1,0:T(8,128)(2,1)} %bitcast.24), custom_call_target="tpu_custom_call" | custom-call | tf_op jit(solution)/shard_map/pallas_call | solution.py:495
  183.4 1.8 broadcast_select_fusion
  (3 shorter events, 0.1 us)
Async XLA Ops:
  5.3 2.4 %copy-start = (bf16[5,24,2048]{2,1,0:T(8,128)(2,1)}, bf16[5,24,2048]{2,1,0:T(8,128)(2,1)S(1)}, u32[]{:S(2)}) copy-start(bf16[5,24,2048]{2,1,0:T(8,128)(2,1)S(1)} %constant_dynamic-update-slice_fusion.xs) | copy-start | bytes 1474564

commit v3 on v2

--- a/solution.py
+++ b/solution.py
@@ -153,12 +153,15 @@
 
 
 def layer_kernel(
-    xs, wt, wg_h, wu_h, wd_h, out,
-    gath, gath_w, part, late, wg, wu, wd, h0, h1, wcol, d0, d1, rx, ry, sums, zin,
-    loc_sem, wsem, agz_s, agz_r, agl_s, agl_r, rsl_s, rsl_r, rsz_s, rsz_r, cross_s, cross_r,
+    act_a, act_b1, grad_b1, enter_a, enter_grad, act_b2,
+    ra1, rb1, ra2, rb2, ga1, gb1, ga2, gb2, wg_h, wu_h, wd_h, out,
+    gath, gath_w, wt, part, late, wg, wu, wd, h0, h1, wcol, d0, d1, rx, ry, sums, zin,
+    loc_sem, wsem, agz_s, agz_r, agl_s, agl_r, agd_s, agd_r, rsl_s, rsl_r, rsz_s, rsz_r,
+    cross_s, cross_r,
 ):
     sec = lax.axis_index("segment")
     me = lax.axis_index("expert")
+    first = sec == 0
     z = me // Q
     q = me % Q
     x_pos = q % 2
@@ -168,13 +171,13 @@
     qd = Q - 1 - q
     x_peer = z * Q + qx
     y_peer = z * Q + qy
-    width = xs.shape[2]
-    rows = xs.shape[1]
+    rows, width = act_a.shape
     total = Q * Z * rows
     half = width // 2
     lo = pl.ds(0, half)
     hi = pl.ds(half, half)
     hidden = wg.shape[1]
+    W = BIG
 
     def rcopy(src, dst, ssem, rsem, peer, seg=sec):
         return pltpu.make_async_remote_copy(
@@ -193,122 +196,170 @@
         pltpu.make_async_copy(src, dst, wsem.at[i])
         for i, (src, dst) in enumerate(((wg_h, wg), (wu_h, wu), (wd_h, wd)))
     ]
-    for c in w_copies:
-        c.start()
+
+    sources = (
+        (act_a, act_b1), (act_b1, grad_b1), (grad_b1, act_a), (enter_a, enter_grad),
+        (act_b2, act_b2), (late, late), (wt, wt),
+    )
+
+    def by_section(k, fn):
+        one, two = sources[k]
+        if one is two:
+            fn(one)
+        else:
+            pl.when(first)(lambda: fn(one))
+            pl.when(jnp.logical_not(first))(lambda: fn(two))
 
     def buf(k):
         return gath.at[k] if k < BIG else gath_w
 
-    def src(k):
-        return xs.at[k] if k < BIG - 1 else (late if k == BIG - 1 else wt)
-
-    def own_copy(k):
-        return pltpu.make_async_copy(src(k), buf(k).at[q, z], loc_sem.at[k])
-
-    def z_send(k, j):
-        return rcopy(src(k), buf(k).at[q, z], agz_s.at[k, j], agz_r.at[k, j], z_peers[j])
+    def own_copy(k, src):
+        return pltpu.make_async_copy(src, buf(k).at[q, z], loc_sem.at[k])
+
+    def z_send(k, j, src):
+        return rcopy(src, buf(k).at[q, z], agz_s.at[k, j], agz_r.at[k, j], z_peers[j])
 
     def z_recv(k, j):
-        return rcopy(src(k), buf(k).at[q, z_from[j]], agz_s.at[k, j], agz_r.at[k, j], z_peers[j])
-
-    def ag_start(k):
-        own_copy(k).start()
-        for j in range(Z - 1):
-            z_send(k, j).start()
-
-    def lay(k, i, block, cols, peer):
-        ref = buf(k).at[block] if cols is None else buf(k).at[block, :, :, cols]
-        return rcopy(ref, ref, agl_s.at[k, i], agl_r.at[k, i], peer)
-
-    def cols(k, c):
-        return c if k < BIG else None
+        dst = buf(k).at[q, z_from[j]]
+        return rcopy(sources[k][0], dst, agz_s.at[k, j], agz_r.at[k, j], z_peers[j])
+
+    def start_z(k):
+        def go(src):
+            own_copy(k, src).start()
+            for j in range(Z - 1):
+                z_send(k, j, src).start()
+
+        by_section(k, go)
+
+    def lay(k, axis, i, block, zz, src=None):
+        ref = buf(k).at[block, zz]
+        peer = x_peer if axis == 0 else y_peer
+        return rcopy(
+            ref if src is None else src, ref, agl_s.at[k, axis, i], agl_r.at[k, axis, i], peer
+        )
+
+    def start_near(k):
+        def go(src):
+            lay(k, 0, Z - 1, q, z, src).start()
+            lay(k, 1, Z - 1, q, z, src).start()
+
+        by_section(k, go)
 
     def l1(k):
-        own_copy(k).wait()
         for j in range(Z - 1):
             z_recv(k, j).wait_recv()
-        lay(k, 0, q, None, x_peer).start()
-        lay(k, 1, q, None, y_peer).start()
+            lay(k, 0, j, q, z_from[j]).start()
+            lay(k, 1, j, q, z_from[j]).start()
+
+    def diag(k, i, block):
+        if k == W:
+            ref = buf(k).at[block]
+        else:
+            ref = buf(k).at[block, :, :, lo if i == 0 else hi]
+        return rcopy(ref, ref, agd_s.at[k, i], agd_r.at[k, i], y_peer if i == 0 else x_peer)
+
+    def near_wait(k, axis):
+        block = qx if axis == 0 else qy
+        for j in range(Z - 1):
+            lay(k, axis, j, block, z_from[j]).wait_recv()
+        lay(k, axis, Z - 1, block, z).wait_recv()
 
     def l2(k):
-        lay(k, 0, qx, None, x_peer).wait_recv()
-        lay(k, 2, qx, cols(k, lo), y_peer).start()
-        lay(k, 1, qy, None, y_peer).wait_recv()
-        if k < BIG:
-            lay(k, 3, qy, hi, x_peer).start()
+        near_wait(k, 0)
+        diag(k, 0, qx).start()
+        near_wait(k, 1)
+        if k != W:
+            diag(k, 1, qy).start()
 
     def arrived(k):
-        lay(k, 2, qd, cols(k, lo), y_peer).wait_recv()
-        if k < BIG:
-            lay(k, 3, qd, hi, x_peer).wait_recv()
+        own_copy(k, sources[k][0]).wait()
+        diag(k, 0, qd).wait_recv()
+        if k != W:
+            diag(k, 1, qd).wait_recv()
 
     def ag_drain(k):
         for j in range(Z - 1):
-            z_send(k, j).wait_send()
-        lay(k, 0, q, None, x_peer).wait_send()
-        lay(k, 1, q, None, y_peer).wait_send()
-        lay(k, 2, qx, cols(k, lo), y_peer).wait_send()
-        if k < BIG:
-            lay(k, 3, qy, hi, x_peer).wait_send()
-
-    def rs_copies(j):
-        def one(i, s, d, peer):
-            return rcopy(s, d, rsl_s.at[j, i], rsl_r.at[j, i], peer)
-
-        return (
-            one(0, part.at[j, qd, :, :, lo], d0.at[j], x_peer),
-            one(1, part.at[j, qd, :, :, hi], d1.at[j], y_peer),
-            one(2, part.at[j, qx], rx.at[j], x_peer),
-            one(3, part.at[j, qy], ry.at[j], y_peer),
+            z_send(k, j, sources[k][0]).wait_send()
+            lay(k, 0, j, q, z_from[j]).wait_send()
+            lay(k, 1, j, q, z_from[j]).wait_send()
+        lay(k, 0, Z - 1, q, z).wait_send()
+        lay(k, 1, Z - 1, q, z).wait_send()
+        diag(k, 0, qx).wait_send()
+        if k != W:
+            diag(k, 1, qy).wait_send()
+
+    def rs(j, i):
+        s, d, peer = (
+            lambda: (part.at[j, qd, :, :, lo], d0.at[j], x_peer),
+            lambda: (part.at[j, qx, :, :, lo], rx.at[j, :, :, lo], x_peer),
+            lambda: (part.at[j, qd, :, :, hi], d1.at[j], y_peer),
+            lambda: (part.at[j, qy, :, :, hi], ry.at[j, :, :, hi], y_peer),
+            lambda: (part.at[j, qy, :, :, lo], ry.at[j, :, :, lo], y_peer),
+            lambda: (part.at[j, qx, :, :, hi], rx.at[j, :, :, hi], x_peer),
+        )[i]()
+        return rcopy(s, d, rsl_s.at[j, i], rsl_r.at[j, i], peer)
+
+    def rs_z(j, i, h):
+        c = hi if h else lo
+        return rcopy(
+            sums.at[j, z_peers[i] // Q, :, c], zin.at[j, i, :, c],
+            rsz_s.at[j, i, h], rsz_r.at[j, i, h], z_peers[i],
         )
 
-    def rs_z(j, i):
-        return rcopy(
-            sums.at[j, z_peers[i] // Q], zin.at[j, i], rsz_s.at[j, i], rsz_r.at[j, i], z_peers[i]
-        )
-
-    def s1(j):
-        a, b, _, _ = rs_copies(j)
-        a.start()
-        b.start()
-
-    def s2(j):
-        a, b, c, d = rs_copies(j)
-        a.wait_recv()
+    def sa(j):
+        rs(j, 0).start()
+        rs(j, 1).start()
+
+    def sb(j):
+        rs(j, 2).start()
+        rs(j, 3).start()
+
+    def s2a(j):
+        rs(j, 0).wait_recv()
         part[j, qy, :, :, lo] = (
             part[j, qy, :, :, lo].astype(F32) + d0[j].astype(F32)
         ).astype(BF16)
-        d.start()
-        b.wait_recv()
+        rs(j, 4).start()
+
+    def s2b(j):
+        rs(j, 2).wait_recv()
         part[j, qx, :, :, hi] = (
             part[j, qx, :, :, hi].astype(F32) + d1[j].astype(F32)
         ).astype(BF16)
-        c.start()
-
-    def s3(j):
-        _, _, c, d = rs_copies(j)
-        c.wait_recv()
-        d.wait_recv()
+        rs(j, 5).start()
+
+    def s3(j, h):
+        for i in ((3, 5) if h else (1, 4)):
+            rs(j, i).wait_recv()
+        c = hi if h else lo
         for i in range(Z - 1):
             zz = z_peers[i] // Q
-            sums[j, zz] = (
-                part[j, q, zz].astype(F32) + rx[j, zz].astype(F32) + ry[j, zz].astype(F32)
+            sums[j, zz, :, c] = (
+                part[j, q, zz, :, c].astype(F32)
+                + rx[j, zz, :, c].astype(F32)
+                + ry[j, zz, :, c].astype(F32)
             ).astype(BF16)
-            rs_z(j, i).start()
+            rs_z(j, i, h).start()
 
     def fin(j):
+        for h, c in enumerate((lo, hi)):
+            for i in range(Z - 1):
+                rs_z(j, i, h).wait_recv()
+            acc = (
+                part[j, q, z, :, c].astype(F32)
+                + rx[j, z, :, c].astype(F32)
+                + ry[j, z, :, c].astype(F32)
+            )
+            for i in range(Z - 1):
+                acc = acc + zin[j, i, :, c].astype(F32)
+            out[j, :, c] = acc.astype(BF16)
+
+    def rs_drain(j):
+        for i in range(6):
+            rs(j, i).wait_send()
         for i in range(Z - 1):
-            rs_z(j, i).wait_recv()
-        acc = part[j, q, z].astype(F32) + rx[j, z].astype(F32) + ry[j, z].astype(F32)
-        for i in range(Z - 1):
-            acc = acc + zin[j, i].astype(F32)
-        out[j] = acc.astype(BF16)
-
-    def rs_drain(j):
-        for c in rs_copies(j):
-            c.wait_send()
-        for i in range(Z - 1):
-            rs_z(j, i).wait_send()
+            rs_z(j, i, 0).wait_send()
+            rs_z(j, i, 1).wait_send()
 
     def crossing():
         return rcopy(out.at[0], late, cross_s, cross_r, me, 1 - sec)
@@ -316,138 +367,147 @@
     def tile(n):
         return pl.ds(pl.multiple_of(n * TILE, TILE), TILE)
 
-    def part_a(j, is_f):
+    def gate_table():
+        lane = lax.broadcasted_iota(jnp.int32, (rows, LANES), 1)
+        routes = (ra1, rb1, ra2, rb2)
+        gates = (ga1, gb1, ga2, gb2)
+        acc = jnp.zeros((rows, LANES), F32)
+        for j in range(JOBS):
+            r = jnp.where(first, routes[j][...], routes[j ^ 1][...]).T
+            g = jnp.where(first, gates[j][...], gates[j ^ 1][...]).T
+            for k in range(r.shape[1]):
+                hit = lane == r[:, k:k + 1] + j * (Q * Z)
+                acc = acc + jnp.where(hit, g[:, k:k + 1], 0.0)
+        wt[...] = acc
+
+    def column(j):
         lane = lax.broadcasted_iota(jnp.int32, (total, LANES), 1)
         table = gath_w[...].reshape(total, LANES)
         picked = jnp.sum(jnp.where(lane == j * (Q * Z) + me, table, 0.0), axis=1, keepdims=True)
         wcol[...] = jnp.broadcast_to(picked, (total, LANES))
 
+    def a_tile(j, n, is_f):
         @pl.when(is_f)
         def _():
-            xi = j + (j + 1) // 2
-
-            def body(n, carry):
-                x = gath[xi].reshape(total, width)
-                g = jnp.dot(x, wg[:, tile(n)], preferred_element_type=F32)
-                u = jnp.dot(x, wu[:, tile(n)], preferred_element_type=F32)
-                h0[:, tile(n)] = (g * jax.nn.sigmoid(g) * u).astype(BF16)
-                return carry
-
-            lax.fori_loop(0, hidden // TILE, body, 0)
+            x = gath[j + (j + 1) // 2].reshape(total, width)
+            g = jnp.dot(x, wg[:, tile(n)], preferred_element_type=F32)
+            u = jnp.dot(x, wu[:, tile(n)], preferred_element_type=F32)
+            h0[:, tile(n)] = (g * jax.nn.sigmoid(g) * u).astype(BF16)
 
         @pl.when(jnp.logical_not(is_f))
         def _():
-            xi = jnp.where(j >= 2, 4, j)
-            ci = j + 1 + j // 3
-
-            def body(n, carry):
-                x = gath[xi].reshape(total, width)
-                c = gath[ci].reshape(total, width)
-                g = jnp.dot(x, wg[:, tile(n)], preferred_element_type=F32)
-                u = jnp.dot(x, wu[:, tile(n)], preferred_element_type=F32)
-                dh = nt_dot(c, wd[tile(n), :])
-                sig = jax.nn.sigmoid(g)
-                h0[:, tile(n)] = (dh * u * sig * (1.0 + g * (1.0 - sig))).astype(BF16)
-                h1[:, tile(n)] = (dh * g * sig).astype(BF16)
-                return carry
-
-            lax.fori_loop(0, hidden // TILE, body, 0)
-
-    def part_b(j, is_f):
-        def put(n, o):
+            x = gath[jnp.where(j >= 2, 4, j)].reshape(total, width)
+            c = gath[j + 1 + j // 3].reshape(total, width)
+            g = jnp.dot(x, wg[:, tile(n)], preferred_element_type=F32)
+            u = jnp.dot(x, wu[:, tile(n)], preferred_element_type=F32)
+            dh = nt_dot(c, wd[tile(n), :])
+            sig = jax.nn.sigmoid(g)
+            h0[:, tile(n)] = (dh * u * sig * (1.0 + g * (1.0 - sig))).astype(BF16)
+            h1[:, tile(n)] = (dh * g * sig).astype(BF16)
+
+    def b_tile(j, n, is_f):
+        def put(o):
             w = jnp.concatenate([wcol[...]] * (TILE // LANES), axis=1)
             part[j, :, :, :, tile(n)] = (o * w).astype(BF16).reshape(Q, Z, rows, TILE)
 
         @pl.when(is_f)
         def _():
-            def body(n, carry):
-                put(n, jnp.dot(h0[...], wd[:, tile(n)], preferred_element_type=F32))
-                return carry
-
-            lax.fori_loop(0, width // TILE, body, 0)
+            put(jnp.dot(h0[...], wd[:, tile(n)], preferred_element_type=F32))
 
         @pl.when(jnp.logical_not(is_f))
         def _():
-            def body(n, carry):
-                put(n, nt_dot(h0[...], wg[tile(n), :]) + nt_dot(h1[...], wu[tile(n), :]))
-                return carry
-
-            lax.fori_loop(0, width // TILE, body, 0)
+            put(nt_dot(h0[...], wg[tile(n), :]) + nt_dot(h1[...], wu[tile(n), :]))
+
+    def run(*steps):
+        def go():
+            for fn, *args in steps:
+                fn(*args)
+
+        return go
+
+    def cross():
+        crossing().start()
+        crossing().wait_recv()
+
+    a_tiles = hidden // TILE
+    b_tiles = width // TILE
+    after_a = {
+        (0, 0): run((l1, 3)),
+        (0, 1): run((l2, 2)),
+        (0, 2): run((start_near, 4), (l1, 4)),
+        (1, 0): run((s2a, 0), (s2b, 0)),
+        (1, 1): run((l2, 3)),
+        (1, 2): run((s3, 0, 0)),
+        (2, 0): run((s2a, 1), (s2b, 1)),
+        (2, 1): run((l1, 5)),
+        (2, 2): run((s3, 1, 0)),
+        (3, 0): run((s2a, 2), (s2b, 2)),
+        (3, 1): run((s3, 2, 0)),
+        (3, 2): run((s3, 2, 1)),
+    }
+    after_b = {
+        (0, 0): run((sa, 0)),
+        (0, 1): run((sb, 0), (arrived, 2)),
+        (1, 0): run((s3, 0, 1), (sa, 1)),
+        (1, 1): run(
+            (sb, 1), (l2, 4), (fin, 0), (cross,), (start_z, 5), (start_near, 5),
+            (arrived, 3), (arrived, 4),
+        ),
+        (2, 0): run((l2, 5), (s3, 1, 1), (sa, 2)),
+        (2, 1): run((sb, 2), (fin, 1), (arrived, 5)),
+        (3, 0): run((sa, 3)),
+        (3, 1): run(
+            (sb, 3), (s2a, 3), (s2b, 3), (fin, 2), (s3, 3, 0), (s3, 3, 1), (fin, 3)
+        ),
+    }
 
     pl.semaphore_wait(barrier, Z + 2)
-    W = BIG
-    for k in (0, 1, W, 2, 3, 4):
-        ag_start(k)
+    start_z(0)
+    start_near(0)
+    start_z(1)
+    start_near(1)
+    gate_table()
+    start_z(W)
+    start_near(W)
+    for k in (2, 3, 4):
+        start_z(k)
+    for c in w_copies:
+        c.start()
     l1(0)
     l1(1)
     l1(W)
     l2(0)
-    l1(2)
+    start_near(2)
     l2(1)
     l2(W)
+    l1(2)
+    start_near(3)
     arrived(0)
     for c in w_copies:
         c.wait()
     arrived(1)
     arrived(W)
 
-    def mid_0():
-        l2(2)
-        l1(3)
-
-    def end_0():
-        s1(0)
-        arrived(2)
-
-    def mid_1():
-        s2(0)
-        l2(3)
-
-    def end_1():
-        s1(1)
-        l1(4)
-        s3(0)
-        arrived(3)
-        s2(1)
-        l2(4)
-        fin(0)
-        crossing().start()
-        crossing().wait_recv()
-        ag_start(5)
-        arrived(4)
-
-    def mid_2():
-        s3(1)
-        l1(5)
-
-    def end_2():
-        s1(2)
-        l2(5)
-        fin(1)
-        s2(2)
-        arrived(5)
-
-    def mid_3():
-        s3(2)
-
-    def end_3():
-        s1(3)
-        s2(3)
-        fin(2)
-        s3(3)
-        fin(3)
-
-    mids = (mid_0, mid_1, mid_2, mid_3)
-    ends = (end_0, end_1, end_2, end_3)
-
     def job(j, carry):
         is_f = (sec + j) % 2 == 0
-        part_a(j, is_f)
-        for i, fn in enumerate(mids):
-            pl.when(j == i)(fn)
-        part_b(j, is_f)
-        for i, fn in enumerate(ends):
-            pl.when(j == i)(fn)
+        column(j)
+
+        def a_step(n, c):
+            a_tile(j, n, is_f)
+            for (jj, nn), fn in after_a.items():
+                at = nn if nn < 2 else a_tiles - 1
+                pl.when((j == jj) & (n == at))(fn)
+            return c
+
+        lax.fori_loop(0, a_tiles, a_step, 0)
+
+        def b_step(n, c):
+            b_tile(j, n, is_f)
+            for (jj, nn), fn in after_b.items():
+                pl.when((j == jj) & (n == (nn + 1) * (b_tiles // 2) - 1))(fn)
+            return c
+
+        lax.fori_loop(0, b_tiles, b_step, 0)
         return carry
 
     lax.fori_loop(0, JOBS, job, 0)
@@ -471,23 +531,6 @@
     def pick(one, two):
         return jnp.where(first, one, two)
 
-    xs = jnp.stack(
-        [
-            pick(act_a[0], act_b1[0]),
-            pick(act_b1[0], grad_b1[0]),
-            pick(grad_b1[0], act_a[0]),
-            pick(enter_a, enter_grad),
-            act_b2[0],
-        ],
-        axis=0,
-    )
-    pairs = ((route_a1, gate_a1), (route_b1, gate_b1), (route_a2, gate_a2), (route_b2, gate_b2))
-    route = jnp.stack([pick(pairs[j][0][0], pairs[j ^ 1][0][0]) for j in range(JOBS)], axis=1)
-    gate = jnp.stack([pick(pairs[j][1][0], pairs[j ^ 1][1][0]) for j in range(JOBS)], axis=1)
-    hit = route[:, :, :, None] == jnp.arange(experts, dtype=jnp.int32)
-    dense = jnp.sum(jnp.where(hit, gate[:, :, :, None], 0.0), axis=2)
-    wt = jnp.pad(dense.reshape(rows, JOBS * experts), ((0, 0), (0, LANES - JOBS * experts)))
-
     vmem = pl.BlockSpec(memory_space=pltpu.VMEM)
     hbm = pl.BlockSpec(memory_space=pl.ANY)
     dma = pltpu.SemaphoreType.DMA
@@ -495,11 +538,12 @@
     done = pl.pallas_call(
         layer_kernel,
         out_shape=jax.ShapeDtypeStruct((JOBS, rows, width), BF16),
-        in_specs=[vmem, vmem, hbm, hbm, hbm],
+        in_specs=[hbm] * 6 + [vmem] * 8 + [hbm] * 3,
         out_specs=vmem,
         scratch_shapes=[
             pltpu.VMEM((BIG, Q, Z, rows, width), BF16),
             pltpu.VMEM((Q, Z, rows, LANES), F32),
+            pltpu.VMEM((rows, LANES), F32),
             pltpu.VMEM((JOBS, Q, Z, rows, width), BF16),
             pltpu.VMEM((rows, width), BF16),
             pltpu.VMEM((width, hidden), BF16),
@@ -516,15 +560,21 @@
             pltpu.VMEM((JOBS, Z - 1, rows, width), BF16),
             dma((BIG + 1,)), dma((3,)),
             dma((BIG + 1, Z - 1)), dma((BIG + 1, Z - 1)),
-            dma((BIG + 1, 4)), dma((BIG + 1, 4)),
-            dma((JOBS, 4)), dma((JOBS, 4)),
-            dma((JOBS, Z - 1)), dma((JOBS, Z - 1)),
+            dma((BIG + 1, 2, Z)), dma((BIG + 1, 2, Z)),
+            dma((BIG + 1, 2)), dma((BIG + 1, 2)),
+            dma((JOBS, 6)), dma((JOBS, 6)),
+            dma((JOBS, Z - 1, 2)), dma((JOBS, Z - 1, 2)),
             dma, dma,
         ],
         compiler_params=pltpu.CompilerParams(
             collective_id=0, has_side_effects=True, vmem_limit_bytes=60 * 1024 * 1024
         ),
-    )(xs, wt, w_gate[0, 0], w_up[0, 0], w_down[0, 0])
+    )(
+        act_a[0], act_b1[0], grad_b1[0], enter_a, enter_grad, act_b2[0],
+        route_a1[0].T, route_b1[0].T, route_a2[0].T, route_b2[0].T,
+        gate_a1[0].T, gate_b1[0].T, gate_a2[0].T, gate_b2[0].T,
+        w_gate[0, 0], w_up[0, 0], w_down[0, 0],
+    )
     fwd_one, grad_one = pick(done[0], done[1]), pick(done[1], done[0])
     fwd_two, grad_two = pick(done[2], done[3]), pick(done[3], done[2])
     return (fwd_one[None], grad_one[None], fwd_two[None], grad_two[None])

time: 186 us -> 164 us (0.88)
  Pallas kernels: 176 us -> 161 us
  other arithmetic: 7.19 us -> 1.8 us
    pallas_call x1, Pallas kernels: 176 us -> 161 us  [fused_shards(): pl.pallas_call(layer_kernel, out_shape=jax.ShapeDtypeStruct((JOBS, rows,...]
    unnamed x4 -> x0, other arithmetic: 3.72 us -> none
where the time goes in v3:
time: 164 us
  Pallas kernels  161 us (98%)
  other arithmetic  1.8 us (1%)
    pallas_call x1, Pallas kernels, fused_shards(): pl.pallas_call(layer_kernel, out_shape=jax.ShapeDtypeStruct((JOBS, rows,...  161 us

profile of v3, /device:TPU:0, one launch (start us, length us, event | category | flops | bytes accessed | tf_op | source)
XLA Modules:
  0.0 163.9 jit_solution(6171056539725624633)
XLA Ops:
  0.6 161.5 %shard_map.192 = bf16[4,24,2048]{2,1,0:T(8,128)(2,1)} custom-call(bf16[24,2048]{1,0:T(8,128)(2,1)} %bitcast.34, bf16[24,2048]{1,0:T(8,128)(2,1)} %bitcast.35, bf16[24,2048]{1,0:T(8,128)(2,1)} %bitcast.36, bf16[24,2048]{1,0:T(8,128)(2,1)} %enter_a.1, bf16[24,2048]{1,0:T(8,128)(2,1)} %enter_grad.1, bf16[24,2048]{1,0:T(8,128)(2,1)} %bitcast.37, ...), custom_call_target="tpu_custom_call" | custom-call | tf_op jit(solution)/shard_map/pallas_call | solution.py:538
  162.1 1.8 %broadcast_select_fusion = (bf16[1,24,2048]{2,1,0:T(8,128)(2,1)}, bf16[1,24,2048]{2,1,0:T(8,128)(2,1)}, bf16[1,24,2048]{2,1,0:T(8,128)(2,1)}, bf16[1,24,2048]{2,1,0:T(8,128)(2,1)}) fusion(pred[]{:T(512)S(6)} %eq.3, bf16[4,24,2048]{2,1,0:T(8,128)(2,1)} %shard_map.192), kind=kLoop, calls=%fused_computation | loop fusion | flops 196608 | bytes 786433 | tf_op jit(solution)/shard_map/jit(_where)/select_n | solution.py:532

commit v4 on v3

--- a/solution.py
+++ b/solution.py
@@ -288,78 +288,82 @@
         if k != W:
             diag(k, 1, qy).wait_send()
 
-    def rs(j, i):
+    quarter = half // 2
+
+    def low(t):
+        return pl.ds(t * quarter, quarter)
+
+    def high(t):
+        return pl.ds(half + t * quarter, quarter)
+
+    def rs(j, i, t):
         s, d, peer = (
-            lambda: (part.at[j, qd, :, :, lo], d0.at[j], x_peer),
-            lambda: (part.at[j, qx, :, :, lo], rx.at[j, :, :, lo], x_peer),
-            lambda: (part.at[j, qd, :, :, hi], d1.at[j], y_peer),
-            lambda: (part.at[j, qy, :, :, hi], ry.at[j, :, :, hi], y_peer),
-            lambda: (part.at[j, qy, :, :, lo], ry.at[j, :, :, lo], y_peer),
-            lambda: (part.at[j, qx, :, :, hi], rx.at[j, :, :, hi], x_peer),
+            lambda: (part.at[j, qd, :, :, low(t)], d0.at[j, :, :, low(t)], x_peer),
+            lambda: (part.at[j, qx, :, :, low(t)], rx.at[j, :, :, low(t)], x_peer),
+            lambda: (part.at[j, qd, :, :, high(t)], d1.at[j, :, :, low(t)], y_peer),
+            lambda: (part.at[j, qy, :, :, high(t)], ry.at[j, :, :, high(t)], y_peer),
+            lambda: (part.at[j, qy, :, :, low(t)], ry.at[j, :, :, low(t)], y_peer),
+            lambda: (part.at[j, qx, :, :, high(t)], rx.at[j, :, :, high(t)], x_peer),
         )[i]()
-        return rcopy(s, d, rsl_s.at[j, i], rsl_r.at[j, i], peer)
-
-    def rs_z(j, i, h):
-        c = hi if h else lo
+        return rcopy(s, d, rsl_s.at[j, i, t], rsl_r.at[j, i, t], peer)
+
+    def rs_z(j, i, t, h):
+        c = high(t) if h else low(t)
         return rcopy(
             sums.at[j, z_peers[i] // Q, :, c], zin.at[j, i, :, c],
-            rsz_s.at[j, i, h], rsz_r.at[j, i, h], z_peers[i],
+            rsz_s.at[j, i, t, h], rsz_r.at[j, i, t, h], z_peers[i],
         )
 
-    def sa(j):
-        rs(j, 0).start()
-        rs(j, 1).start()
-
-    def sb(j):
-        rs(j, 2).start()
-        rs(j, 3).start()
-
-    def s2a(j):
-        rs(j, 0).wait_recv()
-        part[j, qy, :, :, lo] = (
-            part[j, qy, :, :, lo].astype(F32) + d0[j].astype(F32)
+    def s1(j, t):
+        for i in (0, 2, 1, 3):
+            rs(j, i, t).start()
+
+    def s2(j, t):
+        rs(j, 0, t).wait_recv()
+        part[j, qy, :, :, low(t)] = (
+            part[j, qy, :, :, low(t)].astype(F32) + d0[j, :, :, low(t)].astype(F32)
         ).astype(BF16)
-        rs(j, 4).start()
-
-    def s2b(j):
-        rs(j, 2).wait_recv()
-        part[j, qx, :, :, hi] = (
-            part[j, qx, :, :, hi].astype(F32) + d1[j].astype(F32)
+        rs(j, 4, t).start()
+        rs(j, 2, t).wait_recv()
+        part[j, qx, :, :, high(t)] = (
+            part[j, qx, :, :, high(t)].astype(F32) + d1[j, :, :, low(t)].astype(F32)
         ).astype(BF16)
-        rs(j, 5).start()
-
-    def s3(j, h):
-        for i in ((3, 5) if h else (1, 4)):
-            rs(j, i).wait_recv()
-        c = hi if h else lo
-        for i in range(Z - 1):
-            zz = z_peers[i] // Q
-            sums[j, zz, :, c] = (
-                part[j, q, zz, :, c].astype(F32)
-                + rx[j, zz, :, c].astype(F32)
-                + ry[j, zz, :, c].astype(F32)
-            ).astype(BF16)
-            rs_z(j, i, h).start()
+        rs(j, 5, t).start()
+
+    def s3(j, t):
+        for h, c in enumerate((low(t), high(t))):
+            for i in ((3, 5) if h else (1, 4)):
+                rs(j, i, t).wait_recv()
+            for i in range(Z - 1):
+                zz = z_peers[i] // Q
+                sums[j, zz, :, c] = (
+                    part[j, q, zz, :, c].astype(F32)
+                    + rx[j, zz, :, c].astype(F32)
+                    + ry[j, zz, :, c].astype(F32)
+                ).astype(BF16)
+                rs_z(j, i, t, h).start()
 
     def fin(j):
-        for h, c in enumerate((lo, hi)):
+        for t in range(2):
+            for h, c in enumerate((low(t), high(t))):
+                for i in range(Z - 1):
+                    rs_z(j, i, t, h).wait_recv()
+                acc = (
+                    part[j, q, z, :, c].astype(F32)
+                    + rx[j, z, :, c].astype(F32)
+                    + ry[j, z, :, c].astype(F32)
+                )
+                for i in range(Z - 1):
+                    acc = acc + zin[j, i, :, c].astype(F32)
+                out[j, :, c] = acc.astype(BF16)
+
+    def rs_drain(j):
+        for t in range(2):
+            for i in range(6):
+                rs(j, i, t).wait_send()
             for i in range(Z - 1):
-                rs_z(j, i, h).wait_recv()
-            acc = (
-                part[j, q, z, :, c].astype(F32)
-                + rx[j, z, :, c].astype(F32)
-                + ry[j, z, :, c].astype(F32)
-            )
-            for i in range(Z - 1):
-                acc = acc + zin[j, i, :, c].astype(F32)
-            out[j, :, c] = acc.astype(BF16)
-
-    def rs_drain(j):
-        for i in range(6):
-            rs(j, i).wait_send()
-        for i in range(Z - 1):
-            rs_z(j, i, 0).wait_send()
-            rs_z(j, i, 1).wait_send()
+                rs_z(j, i, t, 0).wait_send()
+                rs_z(j, i, t, 1).wait_send()
 
     def crossing():
         return rcopy(out.at[0], late, cross_s, cross_r, me, 1 - sec)
@@ -434,31 +438,26 @@
     after_a = {
         (0, 0): run((l1, 3)),
         (0, 1): run((l2, 2)),
-        (0, 2): run((start_near, 4), (l1, 4)),
-        (1, 0): run((s2a, 0), (s2b, 0)),
-        (1, 1): run((l2, 3)),
-        (1, 2): run((s3, 0, 0)),
-        (2, 0): run((s2a, 1), (s2b, 1)),
-        (2, 1): run((l1, 5)),
+        (0, 2): run((start_near, 4)),
+        (1, 0): run((s2, 0, 1), (l2, 3)),
+        (1, 1): run((s3, 0, 0)),
+        (1, 2): run((s3, 0, 1), (l2, 4)),
+        (2, 0): run((s2, 1, 0)),
+        (2, 1): run((l1, 5), (s2, 1, 1)),
         (2, 2): run((s3, 1, 0)),
-        (3, 0): run((s2a, 2), (s2b, 2)),
+        (3, 0): run((s2, 2, 1)),
         (3, 1): run((s3, 2, 0)),
         (3, 2): run((s3, 2, 1)),
     }
     after_b = {
-        (0, 0): run((sa, 0)),
-        (0, 1): run((sb, 0), (arrived, 2)),
-        (1, 0): run((s3, 0, 1), (sa, 1)),
-        (1, 1): run(
-            (sb, 1), (l2, 4), (fin, 0), (cross,), (start_z, 5), (start_near, 5),
-            (arrived, 3), (arrived, 4),
-        ),
-        (2, 0): run((l2, 5), (s3, 1, 1), (sa, 2)),
-        (2, 1): run((sb, 2), (fin, 1), (arrived, 5)),
-        (3, 0): run((sa, 3)),
-        (3, 1): run(
-            (sb, 3), (s2a, 3), (s2b, 3), (fin, 2), (s3, 3, 0), (s3, 3, 1), (fin, 3)
-        ),
+        (0, 0): run((s1, 0, 0)),
+        (0, 1): run((s1, 0, 1), (s2, 0, 0), (l1, 4), (arrived, 2)),
+        (1, 0): run((s1, 1, 0), (fin, 0), (cross,), (start_z, 5), (start_near, 5)),
+        (1, 1): run((s1, 1, 1), (arrived, 3), (arrived, 4)),
+        (2, 0): run((l2, 5), (s3, 1, 1), (s1, 2, 0)),
+        (2, 1): run((s1, 2, 1), (fin, 1), (s2, 2, 0), (arrived, 5)),
+        (3, 0): run((s1, 3, 0), (fin, 2)),
+        (3, 1): run((s1, 3, 1), (s2, 3, 0), (s2, 3, 1), (s3, 3, 0), (s3, 3, 1), (fin, 3)),
     }
 
     pl.semaphore_wait(barrier, Z + 2)
@@ -502,7 +501,7 @@
         lax.fori_loop(0, a_tiles, a_step, 0)
 
         def b_step(n, c):
-            b_tile(j, n, is_f)
+            b_tile(j, (n % 2) * (b_tiles // 2) + n // 2, is_f)
             for (jj, nn), fn in after_b.items():
                 pl.when((j == jj) & (n == (nn + 1) * (b_tiles // 2) - 1))(fn)
             return c
@@ -562,8 +561,8 @@
             dma((BIG + 1, Z - 1)), dma((BIG + 1, Z - 1)),
             dma((BIG + 1, 2, Z)), dma((BIG + 1, 2, Z)),
             dma((BIG + 1, 2)), dma((BIG + 1, 2)),
-            dma((JOBS, 6)), dma((JOBS, 6)),
-            dma((JOBS, Z - 1, 2)), dma((JOBS, Z - 1, 2)),
+            dma((JOBS, 6, 2)), dma((JOBS, 6, 2)),
+            dma((JOBS, Z - 1, 2, 2)), dma((JOBS, Z - 1, 2, 2)),
             dma, dma,
         ],
         compiler_params=pltpu.CompilerParams(

time: 164 us -> 163 us (level)
  no operation moved by 1% of the time
where the time goes in v4:
time: 163 us
  Pallas kernels  161 us (99%)
  other arithmetic  1.8 us (1%)
    pallas_call x1, Pallas kernels, fused_shards(): pl.pallas_call(layer_kernel, out_shape=jax.ShapeDtypeStruct((JOBS, rows,...  161 us

profile of v4, /device:TPU:0, one launch (start us, length us, event | category | flops | bytes accessed | tf_op | source)
XLA Modules:
  0.0 163.2 jit_solution(12685228041240496406)
XLA Ops:
  0.6 160.7 %shard_map.192 = bf16[4,24,2048]{2,1,0:T(8,128)(2,1)} custom-call(bf16[24,2048]{1,0:T(8,128)(2,1)} %bitcast.34, bf16[24,2048]{1,0:T(8,128)(2,1)} %bitcast.35, bf16[24,2048]{1,0:T(8,128)(2,1)} %bitcast.36, bf16[24,2048]{1,0:T(8,128)(2,1)} %enter_a.1, bf16[24,2048]{1,0:T(8,128)(2,1)} %enter_grad.1, bf16[24,2048]{1,0:T(8,128)(2,1)} %bitcast.37, ...), custom_call_target="tpu_custom_call" | custom-call | tf_op jit(solution)/shard_map/pallas_call | solution.py:537
  161.4 1.8 %broadcast_select_fusion = (bf16[1,24,2048]{2,1,0:T(8,128)(2,1)}, bf16[1,24,2048]{2,1,0:T(8,128)(2,1)}, bf16[1,24,2048]{2,1,0:T(8,128)(2,1)}, bf16[1,24,2048]{2,1,0:T(8,128)(2,1)}) fusion(pred[]{:T(512)S(6)} %eq.3, bf16[4,24,2048]{2,1,0:T(8,128)(2,1)} %shard_map.192), kind=kLoop, calls=%fused_computation | loop fusion | flops 196608 | bytes 786433 | tf_op jit(solution)/shard_map/jit(_where)/select_n | solution.py:531
